TPU v7x, 256 devices: a whole 4x4x8 slice. The times are simulated.
256 devices in a mesh: srow: 32 (over y, x, core), scol: 8 (over z).
Axes of the slice: x: 4, y: 4, z: 8, core: 2. Of those that a mesh axis runs over, the one named last changes fastest.
Arguments:
- factor_state: float32 [32, 512, 4, 8, 512], P('srow', None, None, 'scol'), may hold values from -40 to 40, as said below
- data: float32 [32, 512, 8192], P('srow', None, 'scol'), may hold values from -6 to 6
Outputs:
- factor_out: float32 [32, 512, 4, 8, 512], P('srow', None, None, 'scol')
- data_out: float32 [32, 512, 8192], P('srow', None, 'scol')
Inputs may be any that keep to these rules, and one draw needn't show every extreme that they name: factor_state is exactly symmetric and positive definite as the matrix A.
All inputs are finite; a program needn't handle non-finite values.
Results may differ from a plain program's by a relative error of at most 0.00005.
Values sent between devices are 32-bit elements; how exact they have to be, the bound alone decides.
A program may use at most 128 MiB of HBM per device.

v0:
```python
import jax
import jax.numpy as jnp
from jax import lax
from jax.sharding import Mesh
from jax.sharding import PartitionSpec as P

SROW = ("srow_0", "srow_1", "srow_2")
SROW_SCOL = ("srow_0", "srow_1", "srow_2", "scol")


def spread(shard, axes, root):
    shard = jnp.where(lax.axis_index(axes) == root, shard, jnp.zeros_like(shard))
    for axis in axes:
        shard = lax.psum(shard, axis)
    return shard


def spread_2(value, axis, source):
    kept = jnp.where(lax.axis_index(axis) == source, value, 0).astype(value.dtype)
    return lax.psum(kept, axis)


def per_device(factor_state, data):
    highest = lax.Precision.HIGHEST
    tile_size = factor_state.shape[1]
    groups = factor_state.shape[2]
    col_count = lax.axis_size("scol")
    row_device = lax.axis_index(SROW)
    col_device = lax.axis_index("scol")
    corner = factor_state[0, :, 0, 0, :]
    diagonal = spread(corner, SROW_SCOL, 0)
    lower_tile = jnp.linalg.cholesky(diagonal)
    leading = spread_2(corner, "scol", 0)
    panel_row = jax.scipy.linalg.solve_triangular(lower_tile, leading.T, lower=True).T
    previous = factor_state[0, :, :, 0, :]
    pieces = []
    for column_group in range(groups):
        pieces.append(spread_2(panel_row, SROW, column_group * col_count + col_device))
    stacked = jnp.stack(pieces, axis=0)
    update = jnp.einsum("ac,mbc->amb", panel_row, stacked, precision=highest)
    updated = previous - update
    column_index = jnp.arange(groups, dtype=jnp.int32) * col_count + col_device
    first_column = (column_index == 0)[None, :, None]
    first_row = row_device == 0
    zeros_tiles = jnp.zeros_like(updated)
    top_tiles = jnp.where(first_column, lower_tile[:, None, :], zeros_tiles)
    later_tiles = jnp.where(first_column, panel_row[:, None, :], updated)
    result = jnp.where(first_row, top_tiles, later_tiles)
    factor_out = result.reshape(1, tile_size, groups, 1, tile_size)
    own_data = data[0]
    candidate = jax.scipy.linalg.solve_triangular(lower_tile, own_data, lower=True)
    solved = spread_2(candidate, SROW, 0)
    remain = own_data - jnp.dot(panel_row, solved, precision=highest)
    data_out = jnp.where(first_row, solved, remain)[None]
    return (factor_out, data_out)


def solution(mesh):
    finer = Mesh(
        mesh.devices.reshape(4, 4, 2, mesh.shape["scol"]), ("srow_0", "srow_1", "srow_2", "scol")
    )
    return jax.shard_map(
        per_device,
        mesh=finer,
        in_specs=(P(SROW, None, None, "scol", None), P(SROW, None, "scol")),
        out_specs=(P(SROW, None, None, "scol", None), P(SROW, None, "scol")),
        check_vma=False,
    )
```

profile of v0, /device:TPU:1, one launch (start us, length us, event | category | flops | bytes accessed | tf_op | source)
XLA Modules:
  0.0 558.6 jit_solution(9098768292244726288)
XLA Ops:
  9.7 1.6 select_bitcast_fusion.5
  11.4 53.5 %all-reduce.9.cloned.1.call-done = f32[512,512]{0,1:T(8,128)} async-done(((f32[512,512]{0,1:T(8,128)}), f32[512,512]{0,1:T(8,128)}) %all-reduce.9.cloned.1.call-update) | async-done | bytes 1048592 | tf_op jit(solution)/shard_map/psum | solution.py:14
  64.9 54.2 %all-reduce.11.cloned.1.call-done = f32[512,512]{0,1:T(8,128)} async-done(((f32[512,512]{0,1:T(8,128)}), f32[512,512]{0,1:T(8,128)}) %all-reduce.11.cloned.1.call-update) | async-done | bytes 1048592 | tf_op jit(solution)/shard_map/psum | solution.py:14
  119.2 36.0 %all-reduce.13.cloned.1.call-done = f32[512,512]{0,1:T(8,128)} async-done(((f32[512,512]{0,1:T(8,128)}), f32[512,512]{0,1:T(8,128)}) %all-reduce.13.cloned.1.call-update) | async-done | bytes 1048592 | tf_op jit(solution)/shard_map/psum | solution.py:14
  155.3 82.5 %all-reduce.17.cloned.1.call-done = (f32[512,512]{1,0:T(8,128)}, f32[512,512]{0,1:T(8,128)}) async-done(((f32[512,512]{1,0:T(8,128)}, f32[512,512]{0,1:T(8,128)}), (f32[512,512]{1,0:T(8,128)}, f32[512,512]{0,1:T(8,128)})) %all-reduce.17.cloned.1.call-update) | async-done | bytes 2097168 | tf_op jit(solution)/shard_map/psum | solution.py:20
  237.8 1.6 copy.5
  239.7 11.7 %cholesky.103 = f32[128,128]{1,0:T(8,128)S(1)} custom-call(f32[128,128]{1,0:T(8,128)S(1)} %cholesky.263), custom_call_target="Cholesky" | custom-call | tf_op jit(solution)/shard_map/jit(cholesky)/cholesky | solution.py:32
  251.5 9.8 %custom-call.34 = f32[1,128,128]{1,2,0:T(8,128)S(1)} custom-call(f32[1,128,128]{2,1,0:T(8,128)S(1)} %get-tuple-element.45), custom_call_target="InvertDiagBlocksLowerTriangular" | custom-call | tf_op jit(solution)/shard_map/jit(cholesky)/cholesky | solution.py:32
  262.1 11.7 %cholesky.215 = f32[128,128]{1,0:T(8,128)S(1)} custom-call(f32[128,128]{1,0:T(8,128)S(1)} %cholesky.267), custom_call_target="Cholesky" | custom-call | tf_op jit(solution)/shard_map/jit(cholesky)/cholesky | solution.py:32
  273.8 10.0 %custom-call.35 = f32[1,128,128]{1,2,0:T(8,128)S(1)} custom-call(f32[1,128,128]{2,1,0:T(8,128)S(1)} %get-tuple-element.42), custom_call_target="InvertDiagBlocksLowerTriangular" | custom-call | tf_op jit(solution)/shard_map/jit(cholesky)/cholesky | solution.py:32
  284.5 11.7 %cholesky.236 = f32[128,128]{1,0:T(8,128)S(1)} custom-call(f32[128,128]{1,0:T(8,128)S(1)} %cholesky.272), custom_call_target="Cholesky" | custom-call | tf_op jit(solution)/shard_map/jit(cholesky)/cholesky | solution.py:32
  296.9 9.8 %custom-call.36 = f32[1,128,128]{1,2,0:T(8,128)S(1)} custom-call(f32[1,128,128]{2,1,0:T(8,128)S(1)} %get-tuple-element.39), custom_call_target="InvertDiagBlocksLowerTriangular" | custom-call | tf_op jit(solution)/shard_map/jit(cholesky)/cholesky | solution.py:32
  307.3 11.7 %cholesky.253 = f32[128,128]{1,0:T(8,128)S(1)} custom-call(f32[128,128]{1,0:T(8,128)S(1)} %convolution_subtract_fusion.7), custom_call_target="Cholesky" | custom-call | tf_op jit(solution)/shard_map/jit(cholesky)/cholesky | solution.py:32
  323.0 1.4 fusion.29
  324.4 10.4 %while.1 = (s32[]{:T(128)}, f32[512,512]{1,0:T(8,128)S(1)}, s32[4,2]{0,1:T(2,128)S(1)}, f32[4,128,128]{2,1,0:T(8,128)}, s32[]{:T(128)}) while((s32[]{:T(128)}, f32[512,512]{1,0:T(8,128)S(1)}, s32[4,2]{0,1:T(2,128)S(1)}, f32[4,128,128]{2,1,0:T(8,128)}, s32[]{:T(128)}) %tuple.36), condition=%wide.while_cond, body=%wide.while_body.sunk | while | flops 2 | bytes 132705 | solution.py:34
  325.0 2.0 bitcast_dynamic-update-slice_fusion.2
  327.6 2.0 bitcast_dynamic-update-slice_fusion.2
  330.2 2.0 bitcast_dynamic-update-slice_fusion.2
  332.8 2.0 bitcast_dynamic-update-slice_fusion.2
  334.8 40.2 %custom-call.37 = f32[4,128,128]{1,2,0:T(8,128)S(1)} custom-call(f32[4,128,128]{2,1,0:T(8,128)} %get-tuple-element.9), custom_call_target="InvertDiagBlocksLowerTriangular" | custom-call | tf_op jit(solution)/shard_map/jit(_solve_triangular)/triangular_solve | solution.py:34
  375.0 1.4 fusion.41
  378.1 1.4 convolution_subtract_fusion.2
  380.0 2.6 convolution_subtract_fusion.4
  383.6 1.4 convolution_subtract_fusion.1
  385.7 1.6 convolution_subtract_fusion
  387.9 2.1 fusion.21
  391.3 1.6 maximum_select_fusion
  393.9 1.7 select_bitcast_fusion.3
  396.7 127.9 %all-reduce.15.cloned.1.call-done = (f32[1,512,512]{2,1,0:T(8,128)}, f32[1,512,512]{2,1,0:T(8,128)}, f32[1,512,512]{2,1,0:T(8,128)}, f32[1,512,512]{2,1,0:T(8,128)}, f32[512,1024]{1,0:T(8,128)}) async-done(((f32[1,512,512]{2,1,0:T(8,128)}, f32[1,512,512]{2,1,0:T(8,128)}, f32[1,512,512]{2,1,0:T(8,128)}, f32[1,512,512]{2,1,0:T(8,128)}, f32[512,1024]{1,0:T(8,128)}), (f32[1,512,512]{2,1,0:T(8,128)}, ...) | async-done | bytes 6291472 | tf_op jit(solution)/shard_map/psum | solution.py:20
  524.6 7.2 %fusion.12 = f32[1,512,1024]{2,1,0:T(8,128)} fusion(f32[512,1024]{1,0:T(8,128)} %get-tuple-element.24, f32[1,512,1024]{2,1,0:T(8,128)S(1)} %copy-done, pred[]{:T(512)S(6)} %eq.29, f32[128,512]{0,1:T(8,128)S(1)} %fusion.64, f32[128,512]{0,1:T(8,128)S(1)} %copy.8, f32[128,512]{0,1:T(8,128)S(1)} %copy.7, f32[128,512]{0,1:T(8,128)S(1)} %copy.6), kind=kOutput, calls=%fused_computation.17 | convolution fusion | flops 3223060480 | bytes 7340033 | tf_op jit(solution)/shard_map/dot_general | solution.py:53
  531.8 11.3 %fusion.10 = f32[1,512,4,1,512]{4,1,2,3,0:T(8,128)} fusion(f32[1,512,4,1,512]{4,3,2,1,0:T(1,128)S(1)} %copy-done.3, f32[512,512]{1,0:T(8,128)S(1)} %copy-done.5, f32[512,512]{1,0:T(8,128)S(1)} %copy-done.4, pred[4]{0:T(512)(128)(4,1)S(1)} %add_compare_fusion, pred[]{:T(512)S(6)} %eq.29, f32[1,512,512]{2,1,0:T(8,128)S(1)} %copy-done.7, ...), kind=kOutput, calls=%fused_computation.13 | convolution fusion | flops 6450577408 | bytes 15728645 | tf_op jit(solution)/shard_map/ac,mbc->amb/dot_general | solution.py:40
  543.2 8.5 %copy.11 = f32[1,512,4,1,512]{4,3,2,1,0:T(1,128)} copy(f32[1,512,4,1,512]{4,1,2,3,0:T(8,128)} %fusion.10) | data formatting | bytes 8388608
  (72 shorter events, 17.4 us)
Async XLA Ops:
  7.2 1.2 slice-start
  7.2 57.7 %all-reduce.9.cloned.1.call-start = ((), (), s32[]{:S(2)}) async-start(), calls=%async_computation | async-start | bytes 2097152 | tf_op jit(solution)/shard_map/psum | solution.py:14
  11.4 107.8 %all-reduce.11.cloned.1.call-start = ((), (), s32[]{:S(2)}) async-start(), calls=%async_computation.1 | async-start | bytes 2097152 | tf_op jit(solution)/shard_map/psum | solution.py:14
  64.9 90.3 %all-reduce.13.cloned.1.call-start = ((), (), s32[]{:S(2)}) async-start(), calls=%async_computation.2 | async-start | bytes 2097152 | tf_op jit(solution)/shard_map/psum | solution.py:14
  119.2 118.6 %all-reduce.17.cloned.1.call-start = ((), (), s32[]{:S(2)}) async-start(), calls=%async_computation.4 | async-start | bytes 4194304 | tf_op jit(solution)/shard_map/psum | solution.py:20
  155.2 369.3 %all-reduce.15.cloned.1.call-start = ((), (), s32[]{:S(2)}) async-start(), calls=%async_computation.3 | async-start | bytes 12582912 | tf_op jit(solution)/shard_map/psum | solution.py:20
  237.8 1.7 copy-start.2
  334.8 43.3 %copy-start.1 = (f32[512,512]{1,0:T(8,128)}, f32[512,512]{1,0:T(8,128)S(1)}, u32[]{:S(2)}) copy-start(f32[512,512]{1,0:T(8,128)S(1)} %get-tuple-element.113) | copy-start | bytes 3145732
  379.5 3.4 copy-start
  387.9 2.7 copy-start.6
  524.6 7.3 %copy-start.3 = (f32[1,512,4,1,512]{4,3,2,1,0:T(1,128)S(1)}, f32[1,512,4,1,512]{4,3,2,1,0:T(1,128)}, u32[]{:S(2)}) copy-start(f32[1,512,4,1,512]{4,3,2,1,0:T(1,128)} %param.2) | copy-start | bytes 12582916
  524.6 7.3 %copy-start.4 = (f32[512,512]{1,0:T(8,128)S(1)}, f32[512,512]{1,0:T(8,128)}, u32[]{:S(2)}) copy-start(f32[512,512]{1,0:T(8,128)} %get-tuple-element.28) | copy-start | bytes 3145732
  524.6 7.3 %copy-start.5 = (f32[512,512]{1,0:T(8,128)S(1)}, f32[512,512]{1,0:T(8,128)}, u32[]{:S(2)}) copy-start(f32[512,512]{1,0:T(8,128)} %fusion.49) | copy-start | bytes 3145732
  524.6 7.3 %copy-start.7 = (f32[1,512,512]{2,1,0:T(8,128)S(1)}, f32[1,512,512]{2,1,0:T(8,128)}, u32[]{:S(2)}) copy-start(f32[1,512,512]{2,1,0:T(8,128)} %get-tuple-element.20) | copy-start | bytes 3145732
Sparse Core Ops, SparseCore 0:
  11.5 53.3 all-reduce.8
  67.3 51.7 all-reduce.10
  121.8 33.3 all-reduce.12
  158.2 79.5 all-reduce.16
  395.7 128.7 all-reduce.14
where the time goes:
time: 568 us; the launch traced here: 559 us
  waiting for transfers between devices  354 us (62%)
  other arithmetic  127 us (22%)
  matrix products  36.2 us (6%)
  local copies, waits for them, and re-layouts  23.6 us (4%)
  between operations  17.2 us (3%)
    psum x2, waiting for transfers between devices, spread_2(): return lax.psum(kept, axis)  210 us
    psum x3, waiting for transfers between devices, spread(): shard = lax.psum(shard, axis)  144 us
    another operation x14, other arithmetic, per_device(): lower_tile = jnp.linalg.cholesky(diagonal)  78.6 us
    another operation x3, other arithmetic, per_device(): jax.scipy.linalg.solve_triangular(lower_tile, leading.T, lower=True)  41.6 us
  transfers between devices with their start and end apart: 5, of which 5 were waited for; matrix products, arithmetic and copies ran while one was open for 0% of the time, Pallas kernels for 0%

commit v1 on v0

v1 whole, which is shorter than its diff:
```python
import functools

import jax
import jax.numpy as jnp
from jax import lax
from jax.experimental import pallas as pl
from jax.experimental.pallas import tpu as pltpu
from jax.sharding import PartitionSpec as P

F32 = jnp.float32
BF16 = jnp.bfloat16
HIGHEST = lax.Precision.HIGHEST
MESH = pl.DeviceIdType.MESH
STEPS = ((1, 0), (0, 1), (-1, 0), (0, -1))
DEPTH = (0, 1, 2, 3, 3, 2, 3, 4, 4, 3, 4, 5, 3, 2, 3, 4)
KIDS = ((0, 1, 2, 5, 6, 10, 14), (1, 5), (5, 9, 13), (1, 2, 14))
HOP = 4
CHUNKS = 24


def tdot(a, b):
    return lax.dot_general(a, b, (((0,), (0,)), ((), ())), precision=HIGHEST, preferred_element_type=F32)


def factor_block(s_ref, u_ref):
    sub = lax.broadcasted_iota(jnp.int32, (8, 128), 0)
    row = s_ref[0:8, :]
    before = None
    for k in range(16):
        lo = 8 * k
        last = k == 15
        if before is not None and not last:
            s_ref[lo + 8 : 128, :] = s_ref[lo + 8 : 128, :] - tdot(before[:, lo + 8 : 128], before)
        c = [jnp.broadcast_to(row[:, lo + m : lo + m + 1], (8, 128)) for m in range(8)]
        a = [[jnp.broadcast_to(c[j][i : i + 1, :], (8, 128)) if i >= j else None for j in range(8)] for i in range(8)]
        if not last:
            below = s_ref[lo + 8 : lo + 16, :]
            n = [jnp.broadcast_to(below[:, lo + m : lo + m + 1], (8, 128)) for m in range(8)]
        scale = jnp.zeros((8, 128), F32)
        for j in range(8):
            q = lax.rsqrt(a[j][j])
            r = q * q
            scale = jnp.where(sub == j, q, scale)
            w = [None] * 8
            for i in range(j + 1, 8):
                w[i] = a[i][j] * r
            for i in range(j + 1, 8):
                for m in range(j + 1, i + 1):
                    a[i][m] = a[i][m] - w[i] * a[m][j]
            unit = jnp.where(sub > j, c[j] * r, 0.0)
            for m in range(j + 1, 8):
                c[m] = c[m] - c[j] * w[m]
            pivot = jnp.broadcast_to(row[j : j + 1, :], (8, 256))
            row = row - jnp.concatenate([unit, unit], axis=1) * pivot
            if not last:
                lead = n[j] * r
                for m in range(j + 1, 8):
                    n[m] = n[m] - n[j] * w[m]
                below = below - jnp.concatenate([lead, lead], axis=1) * pivot
        done = row * jnp.concatenate([scale, scale], axis=1)
        u_ref[lo : lo + 8, :] = done
        before = done
        if not last:
            row = below


def factor_step(k, t_ref, s_ref, u_ref):
    rows = lax.broadcasted_iota(jnp.int32, (128, 128), 0)
    cols = lax.broadcasted_iota(jnp.int32, (128, 128), 1)
    base = pl.multiple_of(k * 128, 128)
    mine = pl.ds(base, 128)
    window = pl.ds(base, 640)

    def take(m, carry):
        above = pl.ds(pl.multiple_of(m * 128, 128), 128)
        t_ref[mine, window] = t_ref[mine, window] - tdot(t_ref[above, mine], t_ref[above, window])
        return carry

    lax.fori_loop(0, k, take, 0)
    s_ref[:, 0:128] = t_ref[mine, mine]
    s_ref[:, 128:256] = (rows == cols).astype(F32)
    factor_block(s_ref, u_ref)
    inverse = u_ref[:, 128:256]
    t_ref[mine, mine] = jnp.where(rows <= cols, u_ref[:, 0:128], 0.0)
    t_ref[mine, pl.ds(pl.multiple_of(base + 512, 128), 128)] = inverse
    middle = pl.ds(pl.multiple_of(base + 128, 128), 384)
    t_ref[mine, middle] = jnp.dot(inverse, t_ref[mine, middle], precision=HIGHEST, preferred_element_type=F32)


def gather_kernel(x_hbm, y_hbm, t_out, f_out, y_out, a_out, head, tile, other, hold, t_ref, s_ref, u_ref, sems, tree_recv, z_recv, d_recv, h_recv, t_recv, t_send, tree_send, z_send, d_send, pair_send, pair_recv):
    s = lax.axis_index("srow")
    z = lax.axis_index("scol")
    core = s % 2
    node = s // 2
    x = node % 4
    y = node // 4

    def at(px, py, pcore, pz):
        return (((py % 4) * 4 + px % 4) * 2 + pcore, pz)

    def remote(src, dst, send, recv, device):
        return pltpu.make_async_remote_copy(src_ref=src, dst_ref=dst, send_sem=send, recv_sem=recv, device_id=device, device_id_type=MESH)

    is_root = node == 0
    barrier = pltpu.get_barrier_semaphore()

    @pl.when(core == 1)
    def _():
        t_ref[...] = jnp.zeros_like(t_ref)

    def greet_plane(j, carry):
        pl.semaphore_signal(barrier, inc=1, device_id=((s + j) % 32, z), device_id_type=MESH)
        return carry

    def greet_line(j, carry):
        pl.semaphore_signal(barrier, inc=1, device_id=(s, (z + j) % 8), device_id_type=MESH)
        return carry

    lax.fori_loop(1, 32, greet_plane, 0)
    lax.fori_loop(1, 8, greet_line, 0)

    @pl.when(z == 0)
    def _():
        fetch = pltpu.make_async_copy(x_hbm.at[:, 0:8, :], head, sems.at[0])
        fetch.start()
        fetch.wait()
        for q in range(4):
            tile[:, 128 * q : 128 * q + 128] = head[:, q, :]

    pl.semaphore_wait(barrier, 38)

    def wide(k):
        return slice(128 * k, 512)

    mate = at(x, y, 1 - core, z)

    def flat(ref, n):
        return ref.at[pl.ds(n * 8, 8)]

    @pl.when(core == 1)
    def _():
        @pl.when(z == 0)
        def _():
            remote(tile, other, sems.at[1], sems.at[2], mate).start()
            pltpu.make_async_copy(tile, a_out, sems.at[3]).start()

        def step(k, carry):
            for j in range(4):

                @pl.when(k == j)
                def _():
                    rows = t_ref.at[128 * j : 128 * j + 128, wide(j)]
                    remote(rows, rows, d_send.at[j], d_recv.at[j], mate).wait_recv()

            factor_step(k, t_ref, s_ref, u_ref)
            block = pl.ds(pl.multiple_of(k * 128, 128), 128)
            remote(t_ref.at[block], t_out.at[block], t_send.at[k], t_recv.at[k], mate).start()
            pltpu.make_async_copy(t_ref.at[block], t_out.at[block], t_send.at[k + 4]).start()
            return carry

        lax.fori_loop(0, 4, step, 0)

        def drain(k, carry):
            block = pl.ds(pl.multiple_of(k * 128, 128), 128)
            remote(t_ref.at[block], t_out.at[block], t_send.at[k], t_recv.at[k], mate).wait_send()
            pltpu.make_async_copy(t_ref.at[block], t_out.at[block], t_send.at[k + 4]).wait()
            return carry

        lax.fori_loop(0, 4, drain, 0)
        remote(f_out, f_out, pair_send.at[0], pair_recv.at[0], mate).wait_recv()
        remote(y_out, y_out, pair_send.at[1], pair_recv.at[1], mate).wait_recv()

        @pl.when(z == 0)
        def _():
            remote(tile, other, sems.at[1], sems.at[2], mate).wait_send()
            pltpu.make_async_copy(tile, a_out, sems.at[3]).wait()

        @pl.when(z != 0)
        def _():
            remote(a_out, a_out, pair_send.at[2], pair_recv.at[2], mate).wait_recv()

    @pl.when(core == 0)
    def _():
        @pl.when(jnp.logical_and(is_root, z == 0))
        def _():
            for k in range(4):
                for q, (dx, dy) in enumerate(STEPS):
                    remote(tile.at[pl.ds(128 * k + 32 * q, 32), wide(k)], hold.at[k, :, wide(k)], d_send.at[k], h_recv.at[k], at(dx + 4, dy + 4, 0, 0)).start()

        for q, (dx, dy) in enumerate(STEPS):

            @pl.when(jnp.logical_and(x == dx % 4, y == dy % 4))
            def _():
                for k in range(4):
                    part = hold.at[k, :, wide(k)]
                    rows = pl.ds(128 * k + 32 * q, 32)
                    remote(part, part, d_send.at[k], h_recv.at[k], mate).wait_recv()

                    @pl.when(z == 0)
                    def _():
                        for far in (4, 3, 5, 2, 6, 1, 7):
                            remote(part, part, z_send.at[k + 4], h_recv.at[k], at(x, y, 0, far)).start()

                    def spread(j, carry):
                        remote(part, t_ref.at[rows, wide(k)], d_send.at[k], d_recv.at[k], at(x + (j + 2) % 4, y + (j // 4 + 2) % 4, 1, z)).start()
                        return carry

                    lax.fori_loop(0, 16, spread, 0)

        places = ((x, y), (y, 4 - x), (4 - x, 4 - y), (4 - y, x))
        starts = []
        gives = []
        for t in range(4):
            u = (places[t][1] % 4) * 4 + places[t][0] % 4
            depth = 0
            for n, d in enumerate(DEPTH):
                depth = depth + d * (u == n).astype(jnp.int32)
            starts.append(depth * HOP)
            mine = [None] * 4
            for d in range(4):
                hit = u == KIDS[d][0]
                for n in KIDS[d][1:]:
                    hit = jnp.logical_or(hit, u == n)
                mine[(d + t) % 4] = hit
            gives.append(mine)

        def pieces(t, n):
            return 256 * t + 16 * n, pl.multiple_of(128 * t + 16 * (n - 16), 16)

        def f_copy(src, t, n, send, recv, device):
            block = pl.ds(128 * t + 8 * n, 8)
            return remote(src.at[block], f_out.at[block], send, recv, device)

        def y_copy(src, t, n, send, recv, device):
            block = pl.ds(pl.multiple_of(128 * t + 16 * (n - 16), 16), 16)
            return remote(src.at[block], y_out.at[block], send, recv, device)

        def neighbour(d):
            return at(x + STEPS[d][0] + 4, y + STEPS[d][1] + 4, 0, z)

        def z_rows(i):
            return pl.ds(pl.multiple_of(32 * (i // 2), 32), 32)

        z_depth = jnp.minimum(z, 8 - z)
        z_up = z < 4
        z_down = jnp.logical_or(z == 0, z > 5)

        def z_step(i):
            for k in range(2):

                @pl.when(i % 2 == k)
                def _():
                    rows = z_rows(i)
                    dst = a_out if k == 0 else other

                    def send(src):
                        @pl.when(z_up)
                        def _():
                            remote(src.at[rows], dst.at[rows], z_send.at[k], z_recv.at[i], (s, (z + 1) % 8)).start()

                        @pl.when(z_down)
                        def _():
                            remote(src.at[rows], dst.at[rows], z_send.at[k + 2], z_recv.at[i], (s, (z + 7) % 8)).start()

                    @pl.when(z == 0)
                    def _():
                        send(tile if k == 0 else other)

                    @pl.when(z != 0)
                    def _():
                        remote(dst.at[rows], dst.at[rows], z_send.at[k], z_recv.at[i], mate).wait_recv()
                        send(dst)
                        if k == 1:
                            remote(other.at[rows], a_out.at[rows], pair_send.at[2], pair_recv.at[2], mate).start()

        @pl.when(z == 0)
        def _():
            remote(tile, other, sems.at[1], sems.at[2], mate).wait_recv()
            pltpu.make_async_copy(tile, a_out, sems.at[3]).start()

        def slot(i, carry):
            zi = i - HOP * z_depth

            @pl.when(jnp.logical_and(zi >= 0, zi < 32))
            def _():
                z_step(zi)

            @pl.when(is_root)
            def _():
                for t in range(4):

                    @pl.when(i < 16)
                    def _():
                        f_copy(x_hbm, t, i, tree_send.at[0, t], tree_recv.at[t, i], neighbour(t)).start()
                        f_copy(x_hbm, t, i, pair_send.at[0], pair_recv.at[0], mate).start()

                    @pl.when(jnp.logical_and(i >= 16, i < CHUNKS))
                    def _():
                        y_copy(y_hbm, t, i, tree_send.at[1, t], tree_recv.at[t, i], neighbour(t)).start()
                        y_copy(y_hbm, t, i, pair_send.at[1], pair_recv.at[1], mate).start()

            @pl.when(jnp.logical_not(is_root))
            def _():
                for t in range(4):
                    n = i - starts[t]

                    @pl.when(jnp.logical_and(n >= 0, n < 16))
                    def _():
                        f_copy(f_out, t, n, tree_send.at[0, 0], tree_recv.at[t, n], mate).wait_recv()
                        for d in range(4):

                            @pl.when(gives[t][d])
                            def _():
                                f_copy(f_out, t, n, tree_send.at[0, 4 * t + d], tree_recv.at[t, n], neighbour(d)).start()

                        f_copy(f_out, t, n, pair_send.at[0], pair_recv.at[0], mate).start()

                    @pl.when(jnp.logical_and(n >= 16, n < CHUNKS))
                    def _():
                        y_copy(y_out, t, n, tree_send.at[1, 0], tree_recv.at[t, n], mate).wait_recv()
                        for d in range(4):

                            @pl.when(gives[t][d])
                            def _():
                                y_copy(y_out, t, n, tree_send.at[1, 4 * t + d], tree_recv.at[t, n], neighbour(d)).start()

                        y_copy(y_out, t, n, pair_send.at[1], pair_recv.at[1], mate).start()

            return carry

        lax.fori_loop(0, CHUNKS + 6 * HOP, slot, 0)

        def f_sent(send):
            part = f_out.at[pl.ds(0, 128)]
            remote(part, part, send, pair_recv.at[0], mate).wait_send()

        def y_sent(send):
            part = y_out.at[pl.ds(0, 128)]
            remote(part, part, send, pair_recv.at[1], mate).wait_send()

        @pl.when(is_root)
        def _():
            for t in range(4):
                f_sent(tree_send.at[0, t])
                y_sent(tree_send.at[1, t])

        @pl.when(jnp.logical_not(is_root))
        def _():
            for t in range(4):
                for d in range(4):

                    @pl.when(gives[t][d])
                    def _():
                        f_sent(tree_send.at[0, 4 * t + d])
                        y_sent(tree_send.at[1, 4 * t + d])

        remote(f_out, f_out, pair_send.at[0], pair_recv.at[0], mate).wait_send()
        remote(y_out, y_out, pair_send.at[1], pair_recv.at[1], mate).wait_send()
        for k in range(2):

            @pl.when(z_up)
            def _():
                remote(a_out, a_out, z_send.at[k], pair_recv.at[2], mate).wait_send()

            @pl.when(z_down)
            def _():
                remote(a_out, a_out, z_send.at[k + 2], pair_recv.at[2], mate).wait_send()

        @pl.when(z == 0)
        def _():
            pltpu.make_async_copy(tile, a_out, sems.at[3]).wait()

        @pl.when(z != 0)
        def _():
            remote(a_out, a_out, pair_send.at[2], pair_recv.at[2], mate).wait_send()

        @pl.when(jnp.logical_and(is_root, z == 0))
        def _():
            for k in range(4):
                part = tile.at[0:128, wide(k)]
                remote(part, part, d_send.at[k], h_recv.at[k], mate).wait_send()

        for q, (dx, dy) in enumerate(STEPS):

            @pl.when(jnp.logical_and(x == dx % 4, y == dy % 4))
            def _():
                for k in range(4):
                    part = tile.at[:, wide(k)]
                    remote(part, part, d_send.at[k], h_recv.at[k], mate).wait_send()

                    @pl.when(z == 0)
                    def _():
                        part = tile.at[0:224, wide(k)]
                        remote(part, part, z_send.at[k + 4], h_recv.at[k], mate).wait_send()

        def due(k, carry):
            block = pl.ds(pl.multiple_of(k * 128, 128), 128)
            remote(t_out.at[block], t_out.at[block], t_send.at[k], t_recv.at[k], mate).wait_recv()
            return carry

        lax.fori_loop(0, 4, due, 0)


def gather(x, y):
    dma = pltpu.SemaphoreType.DMA
    anyspace = pl.BlockSpec(memory_space=pl.ANY)
    return pl.pallas_call(
        gather_kernel,
        out_shape=(
            jax.ShapeDtypeStruct((512, 1024), F32),
            jax.ShapeDtypeStruct((512, 16, 128), F32),
            jax.ShapeDtypeStruct((512, 1024), F32),
            jax.ShapeDtypeStruct((512, 512), F32),
        ),
        in_specs=[anyspace] * 2,
        out_specs=[anyspace] * 4,
        scratch_shapes=[
            pltpu.VMEM((512, 8, 128), F32),
            pltpu.VMEM((512, 512), F32),
            pltpu.VMEM((512, 512), F32),
            pltpu.VMEM((4, 32, 512), F32),
            pltpu.VMEM((512, 1024), F32),
            pltpu.VMEM((128, 256), F32),
            pltpu.VMEM((128, 256), F32),
            dma((4,)),
            dma((4, CHUNKS)),
            dma((32,)),
            dma((4,)),
            dma((4,)),
            dma((4,)),
            dma((8,)),
            dma((2, 16)),
            dma((8,)),
            dma((4,)),
            dma((3,)),
            dma((3,)),
        ],
        compiler_params=pltpu.CompilerParams(collective_id=0, has_side_effects=True, vmem_limit_bytes=32 << 20),
        name="gather",
    )(x, y)


def split(v):
    high = v.astype(BF16)
    return high, (v - high.astype(F32)).astype(BF16)


def dot3(a, b):
    ah, al = a
    bh, bl = b
    dot = functools.partial(jnp.dot, preferred_element_type=F32)
    return dot(ah, bh) + (dot(ah, bl) + dot(al, bh))


def update_kernel(t_hbm, f_hbm, r_hbm, a_hbm, x_hbm, y_hbm, fo_hbm, yo_hbm, t, a, f, r, x, y, fo, yo, sems):
    s = lax.axis_index("srow")
    z = lax.axis_index("scol")
    loads = [
        pltpu.make_async_copy(src, dst, sems.at[i])
        for i, (src, dst) in enumerate(((t_hbm, t), (a_hbm, a), (f_hbm, f), (x_hbm, x), (r_hbm, r), (y_hbm, y)))
    ]
    stores = [pltpu.make_async_copy(src, dst, sems.at[6 + i]) for i, (src, dst) in enumerate(((fo, fo_hbm), (yo, yo_hbm)))]
    for load in loads:
        load.start()
    loads[0].wait()
    loads[1].wait()

    def lane(ref, i):
        return ref.at[pl.ds(i, 512, stride=16), :]

    @pl.when(s != 0)
    def _():
        inverse = t[:, 512:1024]
        panel = lax.dot_general(a[...], inverse, (((1,), (1,)), ((), ())), precision=HIGHEST, preferred_element_type=F32)
        q = split(jnp.dot(panel, inverse, precision=HIGHEST, preferred_element_type=F32))
        loads[2].wait()
        loads[3].wait()
        for c in range(4):
            right = split(jnp.concatenate([lane(f, 4 * c + j)[...] for j in range(4)], axis=1))
            change = dot3(q, right)
            for j in range(4):
                lane(fo, 4 * c + j)[...] = lane(x, 4 * c + j)[...] - change[:, 128 * j : 128 * j + 128]

        @pl.when(z == 0)
        def _():
            for j in range(4):
                lane(fo, j)[...] = panel[:, 128 * j : 128 * j + 128]

        stores[0].start()
        loads[4].wait()
        loads[5].wait()
        for c in range(2):
            part = slice(512 * c, 512 * c + 512)
            yo[:, part] = y[:, part] - dot3(q, split(r[:, part]))
        stores[1].start()

    @pl.when(s == 0)
    def _():
        fo[...] = jnp.zeros_like(fo)

        @pl.when(z == 0)
        def _():
            rows = lax.broadcasted_iota(jnp.int32, (512, 512), 0)
            cols = lax.broadcasted_iota(jnp.int32, (512, 512), 1)
            lower = jnp.where(rows >= cols, t[:, 0:512].T, 0.0)
            for j in range(4):
                lane(fo, j)[...] = lower[:, 128 * j : 128 * j + 128]

        stores[0].start()
        for load in loads[2:]:
            load.wait()
        yo[...] = jnp.dot(t[:, 512:1024], y[...], precision=HIGHEST, preferred_element_type=F32)
        stores[1].start()

    stores[0].wait()
    stores[1].wait()


def update(t, f, r, a, x, y):
    anyspace = pl.BlockSpec(memory_space=pl.ANY)
    return pl.pallas_call(
        update_kernel,
        out_shape=(jax.ShapeDtypeStruct((8192, 128), F32), jax.ShapeDtypeStruct((512, 1024), F32)),
        in_specs=[anyspace] * 6,
        out_specs=[anyspace] * 2,
        scratch_shapes=[
            pltpu.VMEM((512, 1024), F32),
            pltpu.VMEM((512, 512), F32),
            pltpu.VMEM((8192, 128), F32),
            pltpu.VMEM((512, 1024), F32),
            pltpu.VMEM((8192, 128), F32),
            pltpu.VMEM((512, 1024), F32),
            pltpu.VMEM((8192, 128), F32),
            pltpu.VMEM((512, 1024), F32),
            pltpu.SemaphoreType.DMA((8,)),
        ],
        compiler_params=pltpu.CompilerParams(vmem_limit_bytes=48 << 20),
        name="update",
    )(t, f, r, a, x, y)


def per_device(factor_state, data):
    x = factor_state.reshape(512, 16, 128)
    y = data.reshape(512, 1024)
    t, f, r, a = gather(x, y)
    factor_out, data_out = update(t, f.reshape(8192, 128), r, a, x.reshape(8192, 128), y)
    return factor_out.reshape(factor_state.shape), data_out.reshape(data.shape)


def solution(mesh):
    specs = (P("srow", None, None, "scol", None), P("srow", None, "scol"))
    return jax.shard_map(per_device, mesh=mesh, in_specs=specs, out_specs=specs, check_vma=False)
```

time: 568 us -> 85.1 us (0.15)
  the two profiles are of different devices: /device:TPU:1 before, /device:TPU:131 now
where the time goes in v1:
time: 85.1 us; the launch traced here: 84.9 us
  Pallas kernels  78.4 us (92%)
  local copies, waits for them, and re-layouts  5.7 us (7%)
    pallas_call x1, Pallas kernels, gather(): pl.pallas_call(gather_kernel, out_shape=(jax.ShapeDtypeStruct((512, 1024)...  65.1 us
    pallas_call x1, Pallas kernels, update(): pl.pallas_call(update_kernel, out_shape=(jax.ShapeDtypeStruct((8192, 128)...  13.3 us
    unnamed x6, local copies, waits for them, and re-layouts  5.7 us

profile of v1, /device:TPU:131, one launch (start us, length us, event | category | flops | bytes accessed | tf_op | source)
XLA Modules:
  0.0 84.9 jit_solution(11331803140600691730)
XLA Ops:
  0.6 0.0 copy-start
  0.6 2.2 %copy-done = f32[1,512,4,1,512]{4,3,2,1,0:T(1,128)S(1)} copy-done((f32[1,512,4,1,512]{4,3,2,1,0:T(1,128)S(1)}, f32[1,512,4,1,512]{4,3,2,1,0:T(1,128)}, u32[]{:S(2)}) %copy-start) | copy-done | bytes 4194328
  2.8 0.0 copy-start.1
  2.8 1.6 %copy-done.1 = f32[1,512,1024]{2,1,0:T(8,128)S(1)} copy-done((f32[1,512,1024]{2,1,0:T(8,128)S(1)}, f32[1,512,1024]{2,1,0:T(8,128)}, u32[]{:S(2)}) %copy-start.1) | copy-done | bytes 2097176
  4.4 65.1 %gather.1 = (f32[512,1024]{1,0:T(8,128)S(1)}, f32[512,16,128]{2,1,0:T(8,128)S(1)}, f32[512,1024]{1,0:T(8,128)S(1)}, f32[512,512]{1,0:T(8,128)S(1)}) custom-call(f32[512,16,128]{2,1,0:T(8,128)S(1)} %bitcast.7, f32[512,1024]{1,0:T(8,128)S(1)} %bitcast.9), custom_call_target="tpu_custom_call" | custom-call | tf_op jit(solution)/shard_map/gather/pallas_call | solution.py:407
  69.5 0.0 copy-start.2
  69.5 1.9 %copy-done.2 = f32[512,16,128]{2,1,0:T(8,128)} copy-done((f32[512,16,128]{2,1,0:T(8,128)}, f32[512,16,128]{2,1,0:T(8,128)S(1)}, u32[]{:S(2)}) %copy-start.2) | copy-done | bytes 4194328
  71.4 13.3 %update.1 = (f32[8192,128]{1,0:T(8,128)}, f32[512,1024]{1,0:T(8,128)}) custom-call(f32[512,1024]{1,0:T(8,128)S(1)} %get-tuple-element.8.t_hbm, f32[8192,128]{1,0:T(8,128)} %bitcast.10, f32[512,1024]{1,0:T(8,128)S(1)} %get-tuple-element.10.r_hbm, f32[512,512]{1,0:T(8,128)S(1)} %get-tuple-element.11.a_hbm, f32[8192,128]{1,0:T(8,128)} %bitcast.6, ...), custom_call_target="tpu_custom_call" | custom-call | tf_op jit(solution)/shard_map/update/pallas_call | solution.py:521
Async XLA Ops:
  0.6 2.2 %copy-start = (f32[1,512,4,1,512]{4,3,2,1,0:T(1,128)S(1)}, f32[1,512,4,1,512]{4,3,2,1,0:T(1,128)}, u32[]{:S(2)}) copy-start(f32[1,512,4,1,512]{4,3,2,1,0:T(1,128)} %param.2) | copy-start | bytes 12582916
  2.8 1.6 %copy-start.1 = (f32[1,512,1024]{2,1,0:T(8,128)S(1)}, f32[1,512,1024]{2,1,0:T(8,128)}, u32[]{:S(2)}) copy-start(f32[1,512,1024]{2,1,0:T(8,128)} %param.3) | copy-start | bytes 6291460
  69.5 1.9 %copy-start.2 = (f32[512,16,128]{2,1,0:T(8,128)}, f32[512,16,128]{2,1,0:T(8,128)S(1)}, u32[]{:S(2)}) copy-start(f32[512,16,128]{2,1,0:T(8,128)S(1)} %get-tuple-element.9) | copy-start | bytes 12582916

commit v2 on v1

v2 whole, which is shorter than its diff:
```python
import functools

import jax
import jax.numpy as jnp
from jax import lax
from jax.experimental import pallas as pl
from jax.experimental.pallas import tpu as pltpu
from jax.sharding import PartitionSpec as P

F32 = jnp.float32
BF16 = jnp.bfloat16
HIGHEST = lax.Precision.HIGHEST
MESH = pl.DeviceIdType.MESH
STEPS = ((1, 0), (0, 1), (-1, 0), (0, -1))
DEPTH = (0, 1, 2, 3, 3, 2, 3, 4, 4, 3, 4, 5, 3, 2, 3, 4)
KIDS = ((0, 1, 2, 5, 6, 10, 14), (1, 5), (5, 9, 13), (1, 2, 14))
HOP = 4
CHUNKS = 24


def tdot(a, b):
    return lax.dot_general(a, b, (((0,), (0,)), ((), ())), precision=HIGHEST, preferred_element_type=F32)


def factor_block(s_ref, u_ref):
    sub = lax.broadcasted_iota(jnp.int32, (8, 128), 0)
    row = s_ref[0:8, :]
    before = None
    for k in range(16):
        lo = 8 * k
        last = k == 15
        if before is not None and not last:
            s_ref[lo + 8 : 128, :] = s_ref[lo + 8 : 128, :] - tdot(before[:, lo + 8 : 128], before)
        c = [jnp.broadcast_to(row[:, lo + m : lo + m + 1], (8, 128)) for m in range(8)]
        a = [[jnp.broadcast_to(c[j][i : i + 1, :], (8, 128)) if i >= j else None for j in range(8)] for i in range(8)]
        if not last:
            below = s_ref[lo + 8 : lo + 16, :]
            n = [jnp.broadcast_to(below[:, lo + m : lo + m + 1], (8, 128)) for m in range(8)]
        scale = jnp.zeros((8, 128), F32)
        for j in range(8):
            q = lax.rsqrt(a[j][j])
            r = q * q
            scale = jnp.where(sub == j, q, scale)
            w = [None] * 8
            for i in range(j + 1, 8):
                w[i] = a[i][j] * r
            for i in range(j + 1, 8):
                for m in range(j + 1, i + 1):
                    a[i][m] = a[i][m] - w[i] * a[m][j]
            unit = jnp.where(sub > j, c[j] * r, 0.0)
            for m in range(j + 1, 8):
                c[m] = c[m] - c[j] * w[m]
            pivot = jnp.broadcast_to(row[j : j + 1, :], (8, 256))
            row = row - jnp.concatenate([unit, unit], axis=1) * pivot
            if not last:
                lead = n[j] * r
                for m in range(j + 1, 8):
                    n[m] = n[m] - n[j] * w[m]
                below = below - jnp.concatenate([lead, lead], axis=1) * pivot
        done = row * jnp.concatenate([scale, scale], axis=1)
        u_ref[lo : lo + 8, :] = done
        before = done
        if not last:
            row = below


def gather_kernel(x_hbm, y_hbm, t_out, f_out, y_out, a_out, head, tile, other, hold, t_ref, s_ref, u_ref, sems, tree_recv, root_recv, z_recv, h_recv, d_recv, t_recv, t_send, r_send, l_send, d_send, c_send, tree_send, root_send, z_send, pair_send, pair_recv):
    s = lax.axis_index("srow")
    z = lax.axis_index("scol")
    core = s % 2
    node = s // 2
    x = node % 4
    y = node // 4
    is_root = node == 0
    is_first = jnp.logical_and(s == 0, z == 0)

    def at(px, py, pcore, pz):
        return (((py % 4) * 4 + px % 4) * 2 + pcore, pz)

    def remote(src, dst, send, recv, device):
        return pltpu.make_async_remote_copy(src_ref=src, dst_ref=dst, send_sem=send, recv_sem=recv, device_id=device, device_id_type=MESH)

    mate = at(x, y, 1 - core, z)
    barrier = pltpu.get_barrier_semaphore()

    def greet_plane(j, carry):
        pl.semaphore_signal(barrier, inc=1, device_id=((s + j) % 32, z), device_id_type=MESH)
        return carry

    def greet_line(j, carry):
        pl.semaphore_signal(barrier, inc=1, device_id=(s, (z + j) % 8), device_id_type=MESH)
        return carry

    lax.fori_loop(1, 32, greet_plane, 0)
    lax.fori_loop(1, 8, greet_line, 0)

    @pl.when(z == 0)
    def _():
        fetch = pltpu.make_async_copy(x_hbm.at[:, 0:8, :], head, sems.at[0])
        fetch.start()
        fetch.wait()
        for q in range(4):
            tile[:, 128 * q : 128 * q + 128] = head[:, q, :]

    pieces = []
    for k in range(4):
        if k:
            pieces.append((k, 0, 128 * k))
        pieces.append((k, 128 * k, 128))

    def piece_rows(k, q):
        return pl.ds(pl.multiple_of(128 * k + 32 * q, 32), 32)

    def lanes(p, shift=0):
        return slice(pieces[p][1] + shift, pieces[p][1] + pieces[p][2] + shift)

    def hand_over():
        for g in range(4):
            for t in range(4):
                block = slice(128 * t + 32 * g, 128 * t + 32 * g + 32)
                copy = remote(x_hbm.at[block], f_out.at[block], pair_send.at[0], root_recv.at[t, g], mate)
                copy.start()
        for g in range(2):
            for t in range(4):
                block = slice(128 * t + 64 * g, 128 * t + 64 * g + 64)
                copy = remote(y_hbm.at[block], y_out.at[block], pair_send.at[1], root_recv.at[t, g + 4], mate)
                copy.start()

    def give_tile():
        remote(tile, other, sems.at[1], sems.at[2], mate).start()
        pltpu.make_async_copy(tile, a_out, sems.at[3]).start()

    @pl.when(is_first)
    def _():
        t_ref[:, 0:512] = tile[...]
        t_ref[:, 512:1024] = jnp.zeros((512, 512), F32)
        rows = lax.broadcasted_iota(jnp.int32, (128, 128), 0)
        cols = lax.broadcasted_iota(jnp.int32, (128, 128), 1)

        def give(p):
            k = pieces[p][0]
            for q, (dx, dy) in enumerate(STEPS):
                remote(t_ref.at[128 * k + 32 * q : 128 * k + 32 * q + 32, lanes(p, 512)], hold.at[k, :, lanes(p)], r_send.at[p], h_recv.at[p], at(dx + 4, dy + 4, 0, 0)).start()

        def given(p):
            part = t_ref.at[0:128, lanes(p, 512)]
            remote(part, part, r_send.at[p], h_recv.at[p], mate).wait_send()

        def step(k, carry):
            base = pl.multiple_of(k * 128, 128)
            mine = pl.ds(base, 128)
            s_ref[:, 0:128] = t_ref[mine, mine]
            s_ref[:, 128:256] = (rows == cols).astype(F32)
            factor_block(s_ref, u_ref)
            inverse = u_ref[:, 128:256]
            t_ref[mine, mine] = jnp.where(rows <= cols, u_ref[:, 0:128], 0.0)
            t_ref[mine, pl.ds(pl.multiple_of(base + 512, 128), 128)] = inverse

            @pl.when(k == 0)
            def _():
                pl.semaphore_wait(barrier, 38)

            for j in range(4):

                @pl.when(k == j)
                def _():
                    give(2 * j)
                    if j:
                        given(2 * j - 1)

            @pl.when(k == 0)
            def _():
                give_tile()
                hand_over()

            middle = pl.ds(pl.multiple_of(base + 128, 128), 384)
            t_ref[mine, middle] = jnp.dot(inverse, t_ref[mine, middle], precision=HIGHEST, preferred_element_type=F32)

            @pl.when(k < 3)
            def _():
                later = pl.multiple_of(base + 128, 128)
                coming = pl.ds(later, 128)
                window = pl.ds(later, 640)

                def take(m, inner):
                    above = pl.ds(pl.multiple_of(m * 128, 128), 128)
                    t_ref[coming, window] = t_ref[coming, window] - tdot(t_ref[above, coming], t_ref[above, window])
                    return inner

                lax.fori_loop(0, k + 1, take, 0)

            for j in range(3):

                @pl.when(k == j)
                def _():
                    give(2 * j + 1)

            return carry

        lax.fori_loop(0, 4, step, 0)
        keep = pltpu.make_async_copy(t_ref.at[:, 0:512], t_out.at[:, 0:512], sems.at[0])
        keep.start()
        for j in range(4):
            given(2 * j)
        keep.wait()

    @pl.when(jnp.logical_not(is_first))
    def _():
        pl.semaphore_wait(barrier, 38)

        @pl.when(z == 0)
        def _():
            give_tile()

        @pl.when(s == 0)
        def _():
            hand_over()

    @pl.when(core == 0)
    def _():
        quarter = jnp.where(x == 1, 0, jnp.where(y == 1, 1, jnp.where(x == 3, 2, 3)))
        holder = jnp.logical_or(jnp.logical_and(y == 0, x % 2 == 1), jnp.logical_and(x == 0, y % 2 == 1))

        @pl.when(holder)
        def _():
            for p, (k, _, _) in enumerate(pieces):
                part = hold.at[k, :, lanes(p)]
                mine = t_out.at[piece_rows(k, quarter), lanes(p, 512)]
                remote(part, part, r_send.at[p], h_recv.at[p], mate).wait_recv()

                @pl.when(z == 0)
                def _():
                    for far in (4, 3, 5, 2, 6, 1, 7):
                        remote(part, part, l_send.at[p], h_recv.at[p], (s, far)).start()

                def around(j, carry):
                    remote(part, mine, d_send.at[p], d_recv.at[p], ((s + 2 * j) % 32, z)).start()
                    return carry

                lax.fori_loop(1, 16, around, 0)
                pltpu.make_async_copy(part, mine, c_send.at[p]).start()

        for p, (k, _, _) in enumerate(pieces):

            @pl.when(holder)
            def _():
                part = t_out.at[0:96, lanes(p, 512)]
                remote(part, part, d_send.at[p], d_recv.at[p], mate).wait_recv()
                pltpu.make_async_copy(hold.at[k, :, lanes(p)], t_out.at[piece_rows(k, quarter), lanes(p, 512)], c_send.at[p]).wait()

            whole = t_out.at[128 * k : 128 * k + 128, lanes(p, 512)]

            @pl.when(jnp.logical_not(holder))
            def _():
                remote(whole, whole, d_send.at[p], d_recv.at[p], mate).wait_recv()

            remote(whole, whole, t_send.at[p], t_recv.at[p], mate).start()

        for p, (k, _, _) in enumerate(pieces):
            whole = t_out.at[128 * k : 128 * k + 128, lanes(p, 512)]
            remote(whole, whole, t_send.at[p], t_recv.at[p], mate).wait_send()

            @pl.when(holder)
            def _():
                part = t_ref.at[0:480, lanes(p)]
                remote(part, part, d_send.at[p], d_recv.at[p], mate).wait_send()

                @pl.when(z == 0)
                def _():
                    part = t_ref.at[0:224, lanes(p)]
                    remote(part, part, l_send.at[p], h_recv.at[p], mate).wait_send()

        @pl.when(z == 0)
        def _():
            remote(tile, other, sems.at[1], sems.at[2], mate).wait_recv()
            remote(tile, other, sems.at[1], sems.at[2], mate).wait_send()
            pltpu.make_async_copy(tile, a_out, sems.at[3]).wait()

        @pl.when(z != 0)
        def _():
            remote(a_out, a_out, pair_send.at[2], pair_recv.at[2], mate).wait_recv()

        @pl.when(is_root)
        def _():
            remote(f_out, f_out, pair_send.at[0], pair_recv.at[0], mate).wait_send()
            remote(y_out, y_out, pair_send.at[1], pair_recv.at[1], mate).wait_send()

        @pl.when(jnp.logical_not(is_root))
        def _():
            remote(f_out, f_out, pair_send.at[0], pair_recv.at[0], mate).wait_recv()
            remote(y_out, y_out, pair_send.at[1], pair_recv.at[1], mate).wait_recv()

    @pl.when(core == 1)
    def _():
        places = ((x, y), (y, 4 - x), (4 - x, 4 - y), (4 - y, x))
        starts = []
        gives = []
        for t in range(4):
            u = (places[t][1] % 4) * 4 + places[t][0] % 4
            depth = 0
            for n, d in enumerate(DEPTH):
                depth = depth + d * (u == n).astype(jnp.int32)
            starts.append(depth * HOP)
            mine = [None] * 4
            for d in range(4):
                hit = u == KIDS[d][0]
                for n in KIDS[d][1:]:
                    hit = jnp.logical_or(hit, u == n)
                mine[(d + t) % 4] = hit
            gives.append(mine)

        def f_copy(t, n, send, recv, device):
            block = f_out.at[pl.ds(128 * t + 8 * n, 8)]
            return remote(block, block, send, recv, device)

        def y_copy(t, n, send, recv, device):
            block = y_out.at[pl.ds(pl.multiple_of(128 * t + 16 * n, 16), 16)]
            return remote(block, block, send, recv, device)

        def neighbour(d):
            return at(x + STEPS[d][0] + 4, y + STEPS[d][1] + 4, 1, z)

        z_depth = jnp.minimum(z, 8 - z)
        z_up = z < 4
        z_down = jnp.logical_or(z == 0, z > 5)

        def z_step(i):
            for k in range(2):

                @pl.when(i % 2 == k)
                def _():
                    rows = pl.ds(pl.multiple_of(32 * (i // 2), 32), 32)
                    dst = a_out if k == 0 else other

                    def send(src):
                        @pl.when(z_up)
                        def _():
                            remote(src.at[rows], dst.at[rows], z_send.at[k], z_recv.at[i], (s, (z + 1) % 8)).start()

                        @pl.when(z_down)
                        def _():
                            remote(src.at[rows], dst.at[rows], z_send.at[k + 2], z_recv.at[i], (s, (z + 7) % 8)).start()

                    @pl.when(z == 0)
                    def _():
                        send(tile if k == 0 else other)

                    @pl.when(z != 0)
                    def _():
                        remote(dst.at[rows], dst.at[rows], z_send.at[k], z_recv.at[i], mate).wait_recv()
                        send(dst)
                        if k == 1:
                            remote(other.at[rows], a_out.at[rows], pair_send.at[2], pair_recv.at[2], mate).start()

        def flow(kind, t, n, copy, total, part):
            @pl.when(is_root)
            def _():
                @pl.when(n % (total // part) == 0)
                def _():
                    if kind == 0:
                        block = f_out.at[0:32]
                    else:
                        block = y_out.at[0:64]
                    remote(block, block, pair_send.at[kind], root_recv.at[t, 4 * kind + n // (total // part)], mate).wait_recv()

                @pl.when(n >= 2)
                def _():
                    copy(t, n, root_send.at[kind, t, n % 2], tree_recv.at[t, n + 16 * kind], neighbour(t)).wait_send()

                copy(t, n, root_send.at[kind, t, n % 2], tree_recv.at[t, n + 16 * kind], neighbour(t)).start()

            @pl.when(jnp.logical_not(is_root))
            def _():
                copy(t, n, tree_send.at[kind, 0], tree_recv.at[t, n + 16 * kind], mate).wait_recv()
                for d in range(4):

                    @pl.when(gives[t][d])
                    def _():
                        copy(t, n, tree_send.at[kind, 4 * t + d], tree_recv.at[t, n + 16 * kind], neighbour(d)).start()

                copy(t, n, pair_send.at[kind], pair_recv.at[kind], mate).start()

        def slot(i, carry):
            for t in range(4):
                n = i - starts[t]

                @pl.when(jnp.logical_and(n >= 0, n < 16))
                def _():
                    flow(0, t, n, f_copy, 16, 4)

                @pl.when(jnp.logical_and(n >= 16, n < CHUNKS))
                def _():
                    flow(1, t, n - 16, y_copy, 8, 2)

            zi = i - HOP * z_depth - 4

            @pl.when(jnp.logical_and(z == 0, zi == 0))
            def _():
                remote(tile, other, sems.at[1], sems.at[2], mate).wait_recv()

            @pl.when(jnp.logical_and(zi >= 0, zi < 32))
            def _():
                z_step(zi)

            return carry

        lax.fori_loop(0, 36 + 4 * HOP, slot, 0)

        f_part = f_out.at[0:128]
        y_part = y_out.at[0:128]

        @pl.when(is_root)
        def _():
            for t in range(4):
                for j in range(2):
                    f_copy(t, j, root_send.at[0, t, j], tree_recv.at[t, 0], mate).wait_send()
                    y_copy(t, j, root_send.at[1, t, j], tree_recv.at[t, 0], mate).wait_send()

        @pl.when(jnp.logical_not(is_root))
        def _():
            for t in range(4):
                for d in range(4):

                    @pl.when(gives[t][d])
                    def _():
                        remote(f_part, f_part, tree_send.at[0, 4 * t + d], pair_recv.at[0], mate).wait_send()
                        remote(y_part, y_part, tree_send.at[1, 4 * t + d], pair_recv.at[1], mate).wait_send()

            remote(f_out, f_out, pair_send.at[0], pair_recv.at[0], mate).wait_send()
            remote(y_out, y_out, pair_send.at[1], pair_recv.at[1], mate).wait_send()

        for k in range(2):

            @pl.when(z_up)
            def _():
                remote(a_out, a_out, z_send.at[k], pair_recv.at[2], mate).wait_send()

            @pl.when(z_down)
            def _():
                remote(a_out, a_out, z_send.at[k + 2], pair_recv.at[2], mate).wait_send()

        @pl.when(z == 0)
        def _():
            remote(tile, other, sems.at[1], sems.at[2], mate).wait_send()
            pltpu.make_async_copy(tile, a_out, sems.at[3]).wait()

        @pl.when(z != 0)
        def _():
            remote(a_out, a_out, pair_send.at[2], pair_recv.at[2], mate).wait_send()

        for p, (k, _, _) in enumerate(pieces):
            whole = t_out.at[128 * k : 128 * k + 128, lanes(p, 512)]
            remote(whole, whole, t_send.at[p], t_recv.at[p], mate).wait_recv()


def gather(x, y):
    dma = pltpu.SemaphoreType.DMA
    anyspace = pl.BlockSpec(memory_space=pl.ANY)
    return pl.pallas_call(
        gather_kernel,
        out_shape=(
            jax.ShapeDtypeStruct((512, 1024), F32),
            jax.ShapeDtypeStruct((512, 16, 128), F32),
            jax.ShapeDtypeStruct((512, 1024), F32),
            jax.ShapeDtypeStruct((512, 512), F32),
        ),
        in_specs=[pl.BlockSpec(memory_space=pltpu.HBM)] * 2,
        out_specs=[anyspace] * 4,
        scratch_shapes=[
            pltpu.VMEM((512, 8, 128), F32),
            pltpu.VMEM((512, 512), F32),
            pltpu.VMEM((512, 512), F32),
            pltpu.VMEM((4, 32, 512), F32),
            pltpu.VMEM((512, 1024), F32),
            pltpu.VMEM((128, 256), F32),
            pltpu.VMEM((128, 256), F32),
            dma((4,)),
            dma((4, CHUNKS)),
            dma((4, 6)),
            dma((32,)),
            dma((7,)),
            dma((7,)),
            dma((7,)),
            dma((7,)),
            dma((7,)),
            dma((7,)),
            dma((7,)),
            dma((7,)),
            dma((2, 16)),
            dma((2, 4, 2)),
            dma((4,)),
            dma((3,)),
            dma((3,)),
        ],
        compiler_params=pltpu.CompilerParams(collective_id=0, has_side_effects=True, vmem_limit_bytes=60 << 20),
        name="gather",
    )(x, y)


def split(v):
    high = v.astype(BF16)
    return high, (v - high.astype(F32)).astype(BF16)


def dot3(a, b, dims=(((1,), (0,)), ((), ()))):
    ah, al = a
    bh, bl = b
    dot = functools.partial(lax.dot_general, dimension_numbers=dims, preferred_element_type=F32)
    return dot(ah, bh) + (dot(ah, bl) + dot(al, bh))


def update_kernel(t_hbm, f_hbm, r_hbm, a_hbm, x_hbm, y_hbm, fo_hbm, yo_hbm, t, a, f, r, x, y, fo, yo, p, q_ref, sems):
    s = lax.axis_index("srow")
    z = lax.axis_index("scol")
    loads = [
        pltpu.make_async_copy(src, dst, sems.at[i])
        for i, (src, dst) in enumerate(((t_hbm, t), (a_hbm, a), (f_hbm, f), (x_hbm, x), (r_hbm, r), (y_hbm, y)))
    ]
    stores = [pltpu.make_async_copy(src, dst, sems.at[6 + i]) for i, (src, dst) in enumerate(((fo, fo_hbm), (yo, yo_hbm)))]
    for load in loads:
        load.start()
    loads[0].wait()
    loads[1].wait()

    def lane(ref, i):
        return ref.at[pl.ds(i, 512, stride=16), :]

    def inverse_rows(k):
        rows = slice(128 * k, 128 * k + 128)
        own = t[rows, 512 + 128 * k : 640 + 128 * k]
        if k == 0:
            return own
        left = jnp.dot(own, t[rows, 512 : 512 + 128 * k], precision=HIGHEST, preferred_element_type=F32)
        return jnp.concatenate([left, own], axis=1)

    @pl.when(s != 0)
    def _():
        al = split(a[...])
        for k in range(4):
            width = 128 * k + 128
            xs = split(inverse_rows(k))
            panel = dot3((al[0][:, :width], al[1][:, :width]), xs, (((1,), (1,)), ((), ())))
            p[:, 128 * k : width] = panel
            add = dot3(split(panel), xs)
            if k:
                q_ref[:, : 128 * k] = q_ref[:, : 128 * k] + add[:, : 128 * k]
            q_ref[:, 128 * k : width] = add[:, 128 * k :]
        q = split(q_ref[...])
        loads[2].wait()
        loads[3].wait()
        for c in range(4):
            right = split(jnp.concatenate([lane(f, 4 * c + j)[...] for j in range(4)], axis=1))
            change = dot3(q, right)
            for j in range(4):
                lane(fo, 4 * c + j)[...] = lane(x, 4 * c + j)[...] - change[:, 128 * j : 128 * j + 128]

        @pl.when(z == 0)
        def _():
            for j in range(4):
                lane(fo, j)[...] = p[:, 128 * j : 128 * j + 128]

        stores[0].start()
        loads[4].wait()
        loads[5].wait()
        for c in range(2):
            part = slice(512 * c, 512 * c + 512)
            yo[:, part] = y[:, part] - dot3(q, split(r[:, part]))
        stores[1].start()

    @pl.when(s == 0)
    def _():
        fo[...] = jnp.zeros_like(fo)

        @pl.when(z == 0)
        def _():
            rows = lax.broadcasted_iota(jnp.int32, (512, 512), 0)
            cols = lax.broadcasted_iota(jnp.int32, (512, 512), 1)
            lower = jnp.where(rows >= cols, t[:, 0:512].T, 0.0)
            for j in range(4):
                lane(fo, j)[...] = lower[:, 128 * j : 128 * j + 128]

        stores[0].start()
        for load in loads[2:]:
            load.wait()
        ys = split(y[...])
        for k in range(4):
            width = 128 * k + 128
            yo[128 * k : width, :] = dot3(split(inverse_rows(k)), (ys[0][:width], ys[1][:width]))
        stores[1].start()

    stores[0].wait()
    stores[1].wait()


def update(t, f, r, a, x, y):
    anyspace = pl.BlockSpec(memory_space=pl.ANY)
    return pl.pallas_call(
        update_kernel,
        out_shape=(jax.ShapeDtypeStruct((8192, 128), F32), jax.ShapeDtypeStruct((512, 1024), F32)),
        in_specs=[anyspace] * 6,
        out_specs=[anyspace] * 2,
        scratch_shapes=[
            pltpu.VMEM((512, 1024), F32),
            pltpu.VMEM((512, 512), F32),
            pltpu.VMEM((8192, 128), F32),
            pltpu.VMEM((512, 1024), F32),
            pltpu.VMEM((8192, 128), F32),
            pltpu.VMEM((512, 1024), F32),
            pltpu.VMEM((8192, 128), F32),
            pltpu.VMEM((512, 1024), F32),
            pltpu.VMEM((512, 512), F32),
            pltpu.VMEM((512, 512), F32),
            pltpu.SemaphoreType.DMA((8,)),
        ],
        compiler_params=pltpu.CompilerParams(vmem_limit_bytes=60 << 20),
        name="update",
    )(t, f, r, a, x, y)


def per_device(factor_state, data):
    x = factor_state.reshape(512, 16, 128)
    y = data.reshape(512, 1024)
    t, f, r, a = gather(x, y)
    factor_out, data_out = update(t, f.reshape(8192, 128), r, a, x.reshape(8192, 128), y)
    return factor_out.reshape(factor_state.shape), data_out.reshape(data.shape)


def solution(mesh):
    specs = (P("srow", None, None, "scol", None), P("srow", None, "scol"))
    return jax.shard_map(per_device, mesh=mesh, in_specs=specs, out_specs=specs, check_vma=False)
```

time: 85.1 us -> 79 us (0.928)
  local copies, waits for them, and re-layouts: 5.7 us -> 0 us
    unnamed x6 -> x0, local copies, waits for them, and re-layouts: 5.7 us -> none
    pallas_call x1, Pallas kernels: 65.1 us -> 62.6 us  [gather(): pl.pallas_call(gather_kernel, out_shape=(jax.ShapeDtypeStruct((512, 1024)...]
    pallas_call x1, Pallas kernels: 13.3 us -> 15.4 us  [update(): pl.pallas_call(update_kernel, out_shape=(jax.ShapeDtypeStruct((8192, 128)...]
where the time goes in v2:
time: 79 us; the launch traced here: 78.9 us
  Pallas kernels  78 us (99%)
  between operations  0.82 us (1%)
    pallas_call x1, Pallas kernels, gather(): pl.pallas_call(gather_kernel, out_shape=(jax.ShapeDtypeStruct((512, 1024)...  62.6 us
    pallas_call x1, Pallas kernels, update(): pl.pallas_call(update_kernel, out_shape=(jax.ShapeDtypeStruct((8192, 128)...  15.4 us

profile of v2, /device:TPU:131, one launch (start us, length us, event | category | flops | bytes accessed | tf_op | source)
XLA Modules:
  0.0 78.9 jit_solution(17770510637380099493)
XLA Ops:
  0.6 62.6 %gather.1 = (f32[512,1024]{1,0:T(8,128)}, f32[512,16,128]{2,1,0:T(8,128)}, f32[512,1024]{1,0:T(8,128)}, f32[512,512]{1,0:T(8,128)}) custom-call(f32[512,16,128]{2,1,0:T(8,128)} %bitcast.6, f32[512,1024]{1,0:T(8,128)} %bitcast.8), custom_call_target="tpu_custom_call" | custom-call | tf_op jit(solution)/shard_map/gather/pallas_call | solution.py:459
  63.3 15.4 %update.1 = (f32[8192,128]{1,0:T(8,128)}, f32[512,1024]{1,0:T(8,128)}) custom-call(f32[512,1024]{1,0:T(8,128)} %get-tuple-element.8.t_hbm, f32[8192,128]{1,0:T(8,128)} %bitcast.10, f32[512,1024]{1,0:T(8,128)} %get-tuple-element.10.r_hbm, f32[512,512]{1,0:T(8,128)} %get-tuple-element.11.a_hbm, f32[8192,128]{1,0:T(8,128)} %bitcast.7, f32[512,1024]{1,0:T(8,128)} %bitcast.9), custom_call_target="tpu_custom_call" | custom-call | tf_op jit(solution)/shard_map/update/pallas_call | solution.py:597

commit v3 on v2

--- a/solution.py
+++ b/solution.py
@@ -64,7 +64,7 @@
             row = below
 
 
-def gather_kernel(x_hbm, y_hbm, t_out, f_out, y_out, a_out, head, tile, other, hold, t_ref, s_ref, u_ref, sems, tree_recv, root_recv, z_recv, h_recv, d_recv, t_recv, t_send, r_send, l_send, d_send, c_send, tree_send, root_send, z_send, pair_send, pair_recv):
+def gather_kernel(x_hbm, y_hbm, t_out, f_out, y_out, a_out, head, tile, other, hold, t_ref, s_ref, u_ref, sems, tree_recv, z_recv, h_recv, d_recv, t_recv, t_send, r_send, l_send, d_send, c_send, tree_send, root_send, z_send, pair_send, pair_recv):
     s = lax.axis_index("srow")
     z = lax.axis_index("scol")
     core = s % 2
@@ -114,17 +114,28 @@
     def lanes(p, shift=0):
         return slice(pieces[p][1] + shift, pieces[p][1] + pieces[p][2] + shift)
 
+    def feed(begin, end):
+        def send(n, carry):
+            for t in range(4):
+                target = at(STEPS[t][0] + 4, STEPS[t][1] + 4, 1, z)
+
+                @pl.when(n < 16)
+                def _():
+                    block = pl.ds(128 * t + 8 * n, 8)
+                    remote(x_hbm.at[block], f_out.at[block], root_send.at[t], tree_recv.at[t, n], target).start()
+
+                @pl.when(n >= 16)
+                def _():
+                    block = pl.ds(pl.multiple_of(128 * t + 16 * (n - 16), 16), 16)
+                    remote(y_hbm.at[block], y_out.at[block], root_send.at[t + 4], tree_recv.at[t, n], target).start()
+
+            return carry
+
+        lax.fori_loop(begin, end, send, 0)
+
     def hand_over():
-        for g in range(4):
-            for t in range(4):
-                block = slice(128 * t + 32 * g, 128 * t + 32 * g + 32)
-                copy = remote(x_hbm.at[block], f_out.at[block], pair_send.at[0], root_recv.at[t, g], mate)
-                copy.start()
-        for g in range(2):
-            for t in range(4):
-                block = slice(128 * t + 64 * g, 128 * t + 64 * g + 64)
-                copy = remote(y_hbm.at[block], y_out.at[block], pair_send.at[1], root_recv.at[t, g + 4], mate)
-                copy.start()
+        remote(x_hbm, f_out, pair_send.at[0], pair_recv.at[0], mate).start()
+        remote(y_hbm, y_out, pair_send.at[1], pair_recv.at[1], mate).start()
 
     def give_tile():
         remote(tile, other, sems.at[1], sems.at[2], mate).start()
@@ -171,6 +182,15 @@
             @pl.when(k == 0)
             def _():
                 give_tile()
+                feed(0, 9)
+
+            @pl.when(k == 1)
+            def _():
+                feed(9, 18)
+
+            @pl.when(k == 2)
+            def _():
+                feed(18, CHUNKS)
                 hand_over()
 
             middle = pl.ds(pl.multiple_of(base + 128, 128), 384)
@@ -214,6 +234,7 @@
 
         @pl.when(s == 0)
         def _():
+            feed(0, CHUNKS)
             hand_over()
 
     @pl.when(core == 0)
@@ -284,6 +305,11 @@
         def _():
             remote(f_out, f_out, pair_send.at[0], pair_recv.at[0], mate).wait_send()
             remote(y_out, y_out, pair_send.at[1], pair_recv.at[1], mate).wait_send()
+            for t in range(4):
+                f_part = f_out.at[0:128]
+                y_part = y_out.at[0:128]
+                remote(f_part, f_part, root_send.at[t], pair_recv.at[0], mate).wait_send()
+                remote(y_part, y_part, root_send.at[t + 4], pair_recv.at[1], mate).wait_send()
 
         @pl.when(jnp.logical_not(is_root))
         def _():
@@ -352,45 +378,27 @@
                         if k == 1:
                             remote(other.at[rows], a_out.at[rows], pair_send.at[2], pair_recv.at[2], mate).start()
 
-        def flow(kind, t, n, copy, total, part):
-            @pl.when(is_root)
-            def _():
-                @pl.when(n % (total // part) == 0)
-                def _():
-                    if kind == 0:
-                        block = f_out.at[0:32]
-                    else:
-                        block = y_out.at[0:64]
-                    remote(block, block, pair_send.at[kind], root_recv.at[t, 4 * kind + n // (total // part)], mate).wait_recv()
-
-                @pl.when(n >= 2)
-                def _():
-                    copy(t, n, root_send.at[kind, t, n % 2], tree_recv.at[t, n + 16 * kind], neighbour(t)).wait_send()
-
-                copy(t, n, root_send.at[kind, t, n % 2], tree_recv.at[t, n + 16 * kind], neighbour(t)).start()
-
-            @pl.when(jnp.logical_not(is_root))
-            def _():
-                copy(t, n, tree_send.at[kind, 0], tree_recv.at[t, n + 16 * kind], mate).wait_recv()
-                for d in range(4):
-
-                    @pl.when(gives[t][d])
-                    def _():
-                        copy(t, n, tree_send.at[kind, 4 * t + d], tree_recv.at[t, n + 16 * kind], neighbour(d)).start()
-
-                copy(t, n, pair_send.at[kind], pair_recv.at[kind], mate).start()
+        def flow(kind, t, n, copy):
+            copy(t, n, tree_send.at[kind, 0], tree_recv.at[t, n + 16 * kind], mate).wait_recv()
+            for d in range(4):
+
+                @pl.when(gives[t][d])
+                def _():
+                    copy(t, n, tree_send.at[kind, 4 * t + d], tree_recv.at[t, n + 16 * kind], neighbour(d)).start()
+
+            copy(t, n, pair_send.at[kind], pair_recv.at[kind], mate).start()
 
         def slot(i, carry):
             for t in range(4):
-                n = i - starts[t]
+                n = jnp.where(is_root, -1, i - starts[t])
 
                 @pl.when(jnp.logical_and(n >= 0, n < 16))
                 def _():
-                    flow(0, t, n, f_copy, 16, 4)
+                    flow(0, t, n, f_copy)
 
                 @pl.when(jnp.logical_and(n >= 16, n < CHUNKS))
                 def _():
-                    flow(1, t, n - 16, y_copy, 8, 2)
+                    flow(1, t, n - 16, y_copy)
 
             zi = i - HOP * z_depth - 4
 
@@ -411,10 +419,8 @@
 
         @pl.when(is_root)
         def _():
-            for t in range(4):
-                for j in range(2):
-                    f_copy(t, j, root_send.at[0, t, j], tree_recv.at[t, 0], mate).wait_send()
-                    y_copy(t, j, root_send.at[1, t, j], tree_recv.at[t, 0], mate).wait_send()
+            remote(f_out, f_out, pair_send.at[0], pair_recv.at[0], mate).wait_recv()
+            remote(y_out, y_out, pair_send.at[1], pair_recv.at[1], mate).wait_recv()
 
         @pl.when(jnp.logical_not(is_root))
         def _():
@@ -476,7 +482,6 @@
             pltpu.VMEM((128, 256), F32),
             dma((4,)),
             dma((4, CHUNKS)),
-            dma((4, 6)),
             dma((32,)),
             dma((7,)),
             dma((7,)),
@@ -487,12 +492,12 @@
             dma((7,)),
             dma((7,)),
             dma((2, 16)),
-            dma((2, 4, 2)),
+            dma((8,)),
             dma((4,)),
             dma((3,)),
             dma((3,)),
         ],
-        compiler_params=pltpu.CompilerParams(collective_id=0, has_side_effects=True, vmem_limit_bytes=60 << 20),
+        compiler_params=pltpu.CompilerParams(collective_id=0, has_side_effects=True, vmem_limit_bytes=53 << 20),
         name="gather",
     )(x, y)
 
@@ -509,7 +514,7 @@
     return dot(ah, bh) + (dot(ah, bl) + dot(al, bh))
 
 
-def update_kernel(t_hbm, f_hbm, r_hbm, a_hbm, x_hbm, y_hbm, fo_hbm, yo_hbm, t, a, f, r, x, y, fo, yo, p, q_ref, sems):
+def update_kernel(t_hbm, f_hbm, r_hbm, a_hbm, x_hbm, y_hbm, fo_hbm, yo_hbm, t, a, f, r, x, y, fo, yo, sems):
     s = lax.axis_index("srow")
     z = lax.axis_index("scol")
     loads = [
@@ -530,22 +535,18 @@
         own = t[rows, 512 + 128 * k : 640 + 128 * k]
         if k == 0:
             return own
-        left = jnp.dot(own, t[rows, 512 : 512 + 128 * k], precision=HIGHEST, preferred_element_type=F32)
+        left = dot3(split(own), split(t[rows, 512 : 512 + 128 * k]))
         return jnp.concatenate([left, own], axis=1)
+
+    def padded_rows(k):
+        rows = inverse_rows(k)
+        return rows if k == 3 else jnp.concatenate([rows, jnp.zeros((128, 384 - 128 * k), F32)], axis=1)
 
     @pl.when(s != 0)
     def _():
-        al = split(a[...])
-        for k in range(4):
-            width = 128 * k + 128
-            xs = split(inverse_rows(k))
-            panel = dot3((al[0][:, :width], al[1][:, :width]), xs, (((1,), (1,)), ((), ())))
-            p[:, 128 * k : width] = panel
-            add = dot3(split(panel), xs)
-            if k:
-                q_ref[:, : 128 * k] = q_ref[:, : 128 * k] + add[:, : 128 * k]
-            q_ref[:, 128 * k : width] = add[:, 128 * k :]
-        q = split(q_ref[...])
+        inverse = split(jnp.concatenate([padded_rows(k) for k in range(4)], axis=0))
+        panel = dot3(split(a[...]), inverse, (((1,), (1,)), ((), ())))
+        q = split(dot3(split(panel), inverse))
         loads[2].wait()
         loads[3].wait()
         for c in range(4):
@@ -557,7 +558,7 @@
         @pl.when(z == 0)
         def _():
             for j in range(4):
-                lane(fo, j)[...] = p[:, 128 * j : 128 * j + 128]
+                lane(fo, j)[...] = panel[:, 128 * j : 128 * j + 128]
 
         stores[0].start()
         loads[4].wait()
@@ -608,11 +609,9 @@
             pltpu.VMEM((512, 1024), F32),
             pltpu.VMEM((8192, 128), F32),
             pltpu.VMEM((512, 1024), F32),
-            pltpu.VMEM((512, 512), F32),
-            pltpu.VMEM((512, 512), F32),
             pltpu.SemaphoreType.DMA((8,)),
         ],
-        compiler_params=pltpu.CompilerParams(vmem_limit_bytes=60 << 20),
+        compiler_params=pltpu.CompilerParams(vmem_limit_bytes=56 << 20),
         name="update",
     )(t, f, r, a, x, y)
 

time: 79 us -> 70.9 us (0.90)
  Pallas kernels: 78 us -> 70 us
    pallas_call x1, Pallas kernels: 62.6 us -> 56.4 us  [gather(): pl.pallas_call(gather_kernel, out_shape=(jax.ShapeDtypeStruct((512, 1024)...]
    pallas_call x1, Pallas kernels: 15.4 us -> 13.6 us  [update(): pl.pallas_call(update_kernel, out_shape=(jax.ShapeDtypeStruct((8192, 128)...]
where the time goes in v3:
time: 70.9 us; the launch traced here: 70.8 us
  Pallas kernels  70 us (99%)
  between operations  0.82 us (1%)
    pallas_call x1, Pallas kernels, gather(): pl.pallas_call(gather_kernel, out_shape=(jax.ShapeDtypeStruct((512, 1024)...  56.4 us
    pallas_call x1, Pallas kernels, update(): pl.pallas_call(update_kernel, out_shape=(jax.ShapeDtypeStruct((8192, 128)...  13.6 us

profile of v3, /device:TPU:131, one launch (start us, length us, event | category | flops | bytes accessed | tf_op | source)
XLA Modules:
  0.0 70.8 jit_solution(956395738604188034)
XLA Ops:
  0.6 56.4 %gather.1 = (f32[512,1024]{1,0:T(8,128)}, f32[512,16,128]{2,1,0:T(8,128)}, f32[512,1024]{1,0:T(8,128)}, f32[512,512]{1,0:T(8,128)}) custom-call(f32[512,16,128]{2,1,0:T(8,128)} %bitcast.6, f32[512,1024]{1,0:T(8,128)} %bitcast.8), custom_call_target="tpu_custom_call" | custom-call | tf_op jit(solution)/shard_map/gather/pallas_call | solution.py:465
  57.0 13.6 %update.1 = (f32[8192,128]{1,0:T(8,128)}, f32[512,1024]{1,0:T(8,128)}) custom-call(f32[512,1024]{1,0:T(8,128)} %get-tuple-element.8.t_hbm, f32[8192,128]{1,0:T(8,128)} %bitcast.10, f32[512,1024]{1,0:T(8,128)} %get-tuple-element.10.r_hbm, f32[512,512]{1,0:T(8,128)} %get-tuple-element.11.a_hbm, f32[8192,128]{1,0:T(8,128)} %bitcast.7, f32[512,1024]{1,0:T(8,128)} %bitcast.9), custom_call_target="tpu_custom_call" | custom-call | tf_op jit(solution)/shard_map/update/pallas_call | solution.py:598

commit v4 on v3

--- a/solution.py
+++ b/solution.py
@@ -14,8 +14,8 @@
 STEPS = ((1, 0), (0, 1), (-1, 0), (0, -1))
 DEPTH = (0, 1, 2, 3, 3, 2, 3, 4, 4, 3, 4, 5, 3, 2, 3, 4)
 KIDS = ((0, 1, 2, 5, 6, 10, 14), (1, 5), (5, 9, 13), (1, 2, 14))
-HOP = 4
-CHUNKS = 24
+HOP = 3
+CHUNKS = 12
 
 
 def tdot(a, b):
@@ -119,14 +119,14 @@
             for t in range(4):
                 target = at(STEPS[t][0] + 4, STEPS[t][1] + 4, 1, z)
 
-                @pl.when(n < 16)
-                def _():
-                    block = pl.ds(128 * t + 8 * n, 8)
+                @pl.when(n < 8)
+                def _():
+                    block = pl.ds(128 * t + 16 * n, 16)
                     remote(x_hbm.at[block], f_out.at[block], root_send.at[t], tree_recv.at[t, n], target).start()
 
-                @pl.when(n >= 16)
-                def _():
-                    block = pl.ds(pl.multiple_of(128 * t + 16 * (n - 16), 16), 16)
+                @pl.when(n >= 8)
+                def _():
+                    block = pl.ds(pl.multiple_of(128 * t + 32 * (n - 8), 32), 32)
                     remote(y_hbm.at[block], y_out.at[block], root_send.at[t + 4], tree_recv.at[t, n], target).start()
 
             return carry
@@ -182,15 +182,15 @@
             @pl.when(k == 0)
             def _():
                 give_tile()
-                feed(0, 9)
+                feed(0, 5)
 
             @pl.when(k == 1)
             def _():
-                feed(9, 18)
+                feed(5, 9)
 
             @pl.when(k == 2)
             def _():
-                feed(18, CHUNKS)
+                feed(9, CHUNKS)
                 hand_over()
 
             middle = pl.ds(pl.multiple_of(base + 128, 128), 384)
@@ -336,11 +336,11 @@
             gives.append(mine)
 
         def f_copy(t, n, send, recv, device):
-            block = f_out.at[pl.ds(128 * t + 8 * n, 8)]
+            block = f_out.at[pl.ds(128 * t + 16 * n, 16)]
             return remote(block, block, send, recv, device)
 
         def y_copy(t, n, send, recv, device):
-            block = y_out.at[pl.ds(pl.multiple_of(128 * t + 16 * n, 16), 16)]
+            block = y_out.at[pl.ds(pl.multiple_of(128 * t + 32 * n, 32), 32)]
             return remote(block, block, send, recv, device)
 
         def neighbour(d):
@@ -355,7 +355,7 @@
 
                 @pl.when(i % 2 == k)
                 def _():
-                    rows = pl.ds(pl.multiple_of(32 * (i // 2), 32), 32)
+                    rows = pl.ds(pl.multiple_of(64 * (i // 2), 64), 64)
                     dst = a_out if k == 0 else other
 
                     def send(src):
@@ -379,12 +379,12 @@
                             remote(other.at[rows], a_out.at[rows], pair_send.at[2], pair_recv.at[2], mate).start()
 
         def flow(kind, t, n, copy):
-            copy(t, n, tree_send.at[kind, 0], tree_recv.at[t, n + 16 * kind], mate).wait_recv()
+            copy(t, n, tree_send.at[kind, 0], tree_recv.at[t, n + 8 * kind], mate).wait_recv()
             for d in range(4):
 
                 @pl.when(gives[t][d])
                 def _():
-                    copy(t, n, tree_send.at[kind, 4 * t + d], tree_recv.at[t, n + 16 * kind], neighbour(d)).start()
+                    copy(t, n, tree_send.at[kind, 4 * t + d], tree_recv.at[t, n + 8 * kind], neighbour(d)).start()
 
             copy(t, n, pair_send.at[kind], pair_recv.at[kind], mate).start()
 
@@ -392,27 +392,27 @@
             for t in range(4):
                 n = jnp.where(is_root, -1, i - starts[t])
 
-                @pl.when(jnp.logical_and(n >= 0, n < 16))
+                @pl.when(jnp.logical_and(n >= 0, n < 8))
                 def _():
                     flow(0, t, n, f_copy)
 
-                @pl.when(jnp.logical_and(n >= 16, n < CHUNKS))
-                def _():
-                    flow(1, t, n - 16, y_copy)
-
-            zi = i - HOP * z_depth - 4
+                @pl.when(jnp.logical_and(n >= 8, n < CHUNKS))
+                def _():
+                    flow(1, t, n - 8, y_copy)
+
+            zi = i - HOP * z_depth - 2
 
             @pl.when(jnp.logical_and(z == 0, zi == 0))
             def _():
                 remote(tile, other, sems.at[1], sems.at[2], mate).wait_recv()
 
-            @pl.when(jnp.logical_and(zi >= 0, zi < 32))
+            @pl.when(jnp.logical_and(zi >= 0, zi < 16))
             def _():
                 z_step(zi)
 
             return carry
 
-        lax.fori_loop(0, 36 + 4 * HOP, slot, 0)
+        lax.fori_loop(0, 18 + 5 * HOP, slot, 0)
 
         f_part = f_out.at[0:128]
         y_part = y_out.at[0:128]
@@ -482,7 +482,7 @@
             pltpu.VMEM((128, 256), F32),
             dma((4,)),
             dma((4, CHUNKS)),
-            dma((32,)),
+            dma((16,)),
             dma((7,)),
             dma((7,)),
             dma((7,)),
@@ -519,13 +519,17 @@
     z = lax.axis_index("scol")
     loads = [
         pltpu.make_async_copy(src, dst, sems.at[i])
-        for i, (src, dst) in enumerate(((t_hbm, t), (a_hbm, a), (f_hbm, f), (x_hbm, x), (r_hbm, r), (y_hbm, y)))
+        for i, (src, dst) in enumerate(((t_hbm.at[:, 512:1024], t.at[:, 512:1024]), (a_hbm, a), (f_hbm, f), (x_hbm, x), (r_hbm, r), (y_hbm, y)))
     ]
-    stores = [pltpu.make_async_copy(src, dst, sems.at[6 + i]) for i, (src, dst) in enumerate(((fo, fo_hbm), (yo, yo_hbm)))]
-    for load in loads:
-        load.start()
+    halves = (slice(0, 512), slice(512, 1024))
+    stores = [pltpu.make_async_copy(fo, fo_hbm, sems.at[6])]
+    stores += [pltpu.make_async_copy(yo.at[:, half], yo_hbm.at[:, half], sems.at[7 + i]) for i, half in enumerate(halves)]
+    loads[0].start()
+    loads[1].start()
     loads[0].wait()
     loads[1].wait()
+    for load in loads[2:]:
+        load.start()
 
     def lane(ref, i):
         return ref.at[pl.ds(i, 512, stride=16), :]
@@ -563,10 +567,9 @@
         stores[0].start()
         loads[4].wait()
         loads[5].wait()
-        for c in range(2):
-            part = slice(512 * c, 512 * c + 512)
+        for c, part in enumerate(halves):
             yo[:, part] = y[:, part] - dot3(q, split(r[:, part]))
-        stores[1].start()
+            stores[1 + c].start()
 
     @pl.when(s == 0)
     def _():
@@ -574,6 +577,9 @@
 
         @pl.when(z == 0)
         def _():
+            upper = pltpu.make_async_copy(t_hbm.at[:, 0:512], t.at[:, 0:512], sems.at[0])
+            upper.start()
+            upper.wait()
             rows = lax.broadcasted_iota(jnp.int32, (512, 512), 0)
             cols = lax.broadcasted_iota(jnp.int32, (512, 512), 1)
             lower = jnp.where(rows >= cols, t[:, 0:512].T, 0.0)
@@ -588,9 +594,10 @@
             width = 128 * k + 128
             yo[128 * k : width, :] = dot3(split(inverse_rows(k)), (ys[0][:width], ys[1][:width]))
         stores[1].start()
-
-    stores[0].wait()
-    stores[1].wait()
+        stores[2].start()
+
+    for store in stores:
+        store.wait()
 
 
 def update(t, f, r, a, x, y):
@@ -609,7 +616,7 @@
             pltpu.VMEM((512, 1024), F32),
             pltpu.VMEM((8192, 128), F32),
             pltpu.VMEM((512, 1024), F32),
-            pltpu.SemaphoreType.DMA((8,)),
+            pltpu.SemaphoreType.DMA((9,)),
         ],
         compiler_params=pltpu.CompilerParams(vmem_limit_bytes=56 << 20),
         name="update",

time: 70.9 us -> 71.4 us (level)
  the two profiles are of different devices: /device:TPU:131 before, /device:TPU:135 now
where the time goes in v4:
time: 71.4 us; the launch traced here: 71.3 us
  Pallas kernels  70.4 us (99%)
  between operations  0.82 us (1%)
    pallas_call x1, Pallas kernels, gather(): pl.pallas_call(gather_kernel, out_shape=(jax.ShapeDtypeStruct((512, 1024)...  56.5 us
    pallas_call x1, Pallas kernels, update(): pl.pallas_call(update_kernel, out_shape=(jax.ShapeDtypeStruct((8192, 128)...  14 us

profile of v4, /device:TPU:135, one launch (start us, length us, event | category | flops | bytes accessed | tf_op | source)
XLA Modules:
  0.0 71.3 jit_solution(2394362596964425087)
XLA Ops:
  0.6 56.5 %gather.1 = (f32[512,1024]{1,0:T(8,128)}, f32[512,16,128]{2,1,0:T(8,128)}, f32[512,1024]{1,0:T(8,128)}, f32[512,512]{1,0:T(8,128)}) custom-call(f32[512,16,128]{2,1,0:T(8,128)} %bitcast.6, f32[512,1024]{1,0:T(8,128)} %bitcast.8), custom_call_target="tpu_custom_call" | custom-call | tf_op jit(solution)/shard_map/gather/pallas_call | solution.py:465
  57.1 14.0 %update.1 = (f32[8192,128]{1,0:T(8,128)}, f32[512,1024]{1,0:T(8,128)}) custom-call(f32[512,1024]{1,0:T(8,128)} %get-tuple-element.8.t_hbm, f32[8192,128]{1,0:T(8,128)} %bitcast.10, f32[512,1024]{1,0:T(8,128)} %get-tuple-element.10.r_hbm, f32[512,512]{1,0:T(8,128)} %get-tuple-element.11.a_hbm, f32[8192,128]{1,0:T(8,128)} %bitcast.7, f32[512,1024]{1,0:T(8,128)} %bitcast.9), custom_call_target="tpu_custom_call" | custom-call | tf_op jit(solution)/shard_map/update/pallas_call | solution.py:605

commit v5 on v3

--- a/solution.py
+++ b/solution.py
@@ -182,15 +182,14 @@
             @pl.when(k == 0)
             def _():
                 give_tile()
-                feed(0, 9)
+                feed(0, 13)
 
             @pl.when(k == 1)
             def _():
-                feed(9, 18)
+                feed(13, CHUNKS)
 
             @pl.when(k == 2)
             def _():
-                feed(18, CHUNKS)
                 hand_over()
 
             middle = pl.ds(pl.multiple_of(base + 128, 128), 384)
@@ -237,11 +236,79 @@
             feed(0, CHUNKS)
             hand_over()
 
+    quarter = jnp.where(x == 1, 0, jnp.where(y == 1, 1, jnp.where(x == 3, 2, 3)))
+    holder = jnp.logical_or(jnp.logical_and(y == 0, x % 2 == 1), jnp.logical_and(x == 0, y % 2 == 1))
+    on_line = core == jnp.logical_or(holder, is_root).astype(jnp.int32)
+
+    z_depth = jnp.minimum(z, 8 - z)
+    z_up = z < 4
+    z_down = jnp.logical_or(z == 0, z > 5)
+
+    def z_step(i):
+        for k in range(2):
+
+            @pl.when(i % 2 == k)
+            def _():
+                rows = pl.ds(pl.multiple_of(32 * (i // 2), 32), 32)
+                dst = a_out if k == 0 else other
+
+                def send(src):
+                    @pl.when(z_up)
+                    def _():
+                        remote(src.at[rows], dst.at[rows], z_send.at[k], z_recv.at[i], (s, (z + 1) % 8)).start()
+
+                    @pl.when(z_down)
+                    def _():
+                        remote(src.at[rows], dst.at[rows], z_send.at[k + 2], z_recv.at[i], (s, (z + 7) % 8)).start()
+
+                @pl.when(z == 0)
+                def _():
+                    send(tile if k == 0 else other)
+
+                @pl.when(z != 0)
+                def _():
+                    remote(dst.at[rows], dst.at[rows], z_send.at[k], z_recv.at[i], mate).wait_recv()
+                    send(dst)
+                    if k == 1:
+                        remote(other.at[rows], a_out.at[rows], pair_send.at[2], pair_recv.at[2], mate).start()
+
+    def tile_came():
+        remote(tile, other, sems.at[1], sems.at[2], mate).wait_recv()
+
+    def line_end():
+        @pl.when(on_line)
+        def _():
+            for k in range(2):
+
+                @pl.when(z_up)
+                def _():
+                    remote(a_out, a_out, z_send.at[k], pair_recv.at[2], mate).wait_send()
+
+                @pl.when(z_down)
+                def _():
+                    remote(a_out, a_out, z_send.at[k + 2], pair_recv.at[2], mate).wait_send()
+
+            @pl.when(z != 0)
+            def _():
+                remote(a_out, a_out, pair_send.at[2], pair_recv.at[2], mate).wait_send()
+
+        @pl.when(jnp.logical_not(on_line))
+        def _():
+            @pl.when(z == 0)
+            def _():
+                tile_came()
+
+            @pl.when(z != 0)
+            def _():
+                remote(a_out, a_out, pair_send.at[2], pair_recv.at[2], mate).wait_recv()
+
+        @pl.when(z == 0)
+        def _():
+            remote(tile, other, sems.at[1], sems.at[2], mate).wait_send()
+            pltpu.make_async_copy(tile, a_out, sems.at[3]).wait()
+
     @pl.when(core == 0)
     def _():
-        quarter = jnp.where(x == 1, 0, jnp.where(y == 1, 1, jnp.where(x == 3, 2, 3)))
-        holder = jnp.logical_or(jnp.logical_and(y == 0, x % 2 == 1), jnp.logical_and(x == 0, y % 2 == 1))
-
         @pl.when(holder)
         def _():
             for p, (k, _, _) in enumerate(pieces):
@@ -261,6 +328,18 @@
                 lax.fori_loop(1, 16, around, 0)
                 pltpu.make_async_copy(part, mine, c_send.at[p]).start()
 
+        @pl.when(on_line)
+        def _():
+            @pl.when(z == 0)
+            def _():
+                tile_came()
+
+            def pass_on(i, carry):
+                z_step(i)
+                return carry
+
+            lax.fori_loop(0, 32, pass_on, 0)
+
         for p, (k, _, _) in enumerate(pieces):
 
             @pl.when(holder)
@@ -291,15 +370,7 @@
                     part = t_ref.at[0:224, lanes(p)]
                     remote(part, part, l_send.at[p], h_recv.at[p], mate).wait_send()
 
-        @pl.when(z == 0)
-        def _():
-            remote(tile, other, sems.at[1], sems.at[2], mate).wait_recv()
-            remote(tile, other, sems.at[1], sems.at[2], mate).wait_send()
-            pltpu.make_async_copy(tile, a_out, sems.at[3]).wait()
-
-        @pl.when(z != 0)
-        def _():
-            remote(a_out, a_out, pair_send.at[2], pair_recv.at[2], mate).wait_recv()
+        line_end()
 
         @pl.when(is_root)
         def _():
@@ -346,38 +417,6 @@
         def neighbour(d):
             return at(x + STEPS[d][0] + 4, y + STEPS[d][1] + 4, 1, z)
 
-        z_depth = jnp.minimum(z, 8 - z)
-        z_up = z < 4
-        z_down = jnp.logical_or(z == 0, z > 5)
-
-        def z_step(i):
-            for k in range(2):
-
-                @pl.when(i % 2 == k)
-                def _():
-                    rows = pl.ds(pl.multiple_of(32 * (i // 2), 32), 32)
-                    dst = a_out if k == 0 else other
-
-                    def send(src):
-                        @pl.when(z_up)
-                        def _():
-                            remote(src.at[rows], dst.at[rows], z_send.at[k], z_recv.at[i], (s, (z + 1) % 8)).start()
-
-                        @pl.when(z_down)
-                        def _():
-                            remote(src.at[rows], dst.at[rows], z_send.at[k + 2], z_recv.at[i], (s, (z + 7) % 8)).start()
-
-                    @pl.when(z == 0)
-                    def _():
-                        send(tile if k == 0 else other)
-
-                    @pl.when(z != 0)
-                    def _():
-                        remote(dst.at[rows], dst.at[rows], z_send.at[k], z_recv.at[i], mate).wait_recv()
-                        send(dst)
-                        if k == 1:
-                            remote(other.at[rows], a_out.at[rows], pair_send.at[2], pair_recv.at[2], mate).start()
-
         def flow(kind, t, n, copy):
             copy(t, n, tree_send.at[kind, 0], tree_recv.at[t, n + 16 * kind], mate).wait_recv()
             for d in range(4):
@@ -400,11 +439,11 @@
                 def _():
                     flow(1, t, n - 16, y_copy)
 
-            zi = i - HOP * z_depth - 4
+            zi = jnp.where(on_line, i - HOP * z_depth - 4, -1)
 
             @pl.when(jnp.logical_and(z == 0, zi == 0))
             def _():
-                remote(tile, other, sems.at[1], sems.at[2], mate).wait_recv()
+                tile_came()
 
             @pl.when(jnp.logical_and(zi >= 0, zi < 32))
             def _():
@@ -435,24 +474,7 @@
             remote(f_out, f_out, pair_send.at[0], pair_recv.at[0], mate).wait_send()
             remote(y_out, y_out, pair_send.at[1], pair_recv.at[1], mate).wait_send()
 
-        for k in range(2):
-
-            @pl.when(z_up)
-            def _():
-                remote(a_out, a_out, z_send.at[k], pair_recv.at[2], mate).wait_send()
-
-            @pl.when(z_down)
-            def _():
-                remote(a_out, a_out, z_send.at[k + 2], pair_recv.at[2], mate).wait_send()
-
-        @pl.when(z == 0)
-        def _():
-            remote(tile, other, sems.at[1], sems.at[2], mate).wait_send()
-            pltpu.make_async_copy(tile, a_out, sems.at[3]).wait()
-
-        @pl.when(z != 0)
-        def _():
-            remote(a_out, a_out, pair_send.at[2], pair_recv.at[2], mate).wait_send()
+        line_end()
 
         for p, (k, _, _) in enumerate(pieces):
             whole = t_out.at[128 * k : 128 * k + 128, lanes(p, 512)]
@@ -521,7 +543,9 @@
         pltpu.make_async_copy(src, dst, sems.at[i])
         for i, (src, dst) in enumerate(((t_hbm, t), (a_hbm, a), (f_hbm, f), (x_hbm, x), (r_hbm, r), (y_hbm, y)))
     ]
-    stores = [pltpu.make_async_copy(src, dst, sems.at[6 + i]) for i, (src, dst) in enumerate(((fo, fo_hbm), (yo, yo_hbm)))]
+    halves = (slice(0, 512), slice(512, 1024))
+    stores = [pltpu.make_async_copy(fo, fo_hbm, sems.at[6])]
+    stores += [pltpu.make_async_copy(yo.at[:, half], yo_hbm.at[:, half], sems.at[7 + i]) for i, half in enumerate(halves)]
     for load in loads:
         load.start()
     loads[0].wait()
@@ -563,10 +587,9 @@
         stores[0].start()
         loads[4].wait()
         loads[5].wait()
-        for c in range(2):
-            part = slice(512 * c, 512 * c + 512)
+        for c, part in enumerate(halves):
             yo[:, part] = y[:, part] - dot3(q, split(r[:, part]))
-        stores[1].start()
+            stores[1 + c].start()
 
     @pl.when(s == 0)
     def _():
@@ -588,9 +611,10 @@
             width = 128 * k + 128
             yo[128 * k : width, :] = dot3(split(inverse_rows(k)), (ys[0][:width], ys[1][:width]))
         stores[1].start()
-
-    stores[0].wait()
-    stores[1].wait()
+        stores[2].start()
+
+    for store in stores:
+        store.wait()
 
 
 def update(t, f, r, a, x, y):
@@ -609,7 +633,7 @@
             pltpu.VMEM((512, 1024), F32),
             pltpu.VMEM((8192, 128), F32),
             pltpu.VMEM((512, 1024), F32),
-            pltpu.SemaphoreType.DMA((8,)),
+            pltpu.SemaphoreType.DMA((9,)),
         ],
         compiler_params=pltpu.CompilerParams(vmem_limit_bytes=56 << 20),
         name="update",

time: 70.9 us -> 70.6 us (level); the launches traced: 70.8 us -> 69.3 us
  Pallas kernels: 70 us -> 68.5 us
    pallas_call x1, Pallas kernels: 56.4 us -> 55.1 us  [gather(): pl.pallas_call(gather_kernel, out_shape=(jax.ShapeDtypeStruct((512, 1024)...]
where the time goes in v5:
time: 70.6 us; the launch traced here: 69.3 us
  Pallas kernels  68.5 us (97%)
  between operations  0.82 us (1%)
    pallas_call x1, Pallas kernels, gather(): pl.pallas_call(gather_kernel, out_shape=(jax.ShapeDtypeStruct((512, 1024)...  55.1 us
    pallas_call x1, Pallas kernels, update(): pl.pallas_call(update_kernel, out_shape=(jax.ShapeDtypeStruct((8192, 128)...  13.3 us

profile of v5, /device:TPU:131, one launch (start us, length us, event | category | flops | bytes accessed | tf_op | source)
XLA Modules:
  0.0 69.3 jit_solution(13810012544890900028)
XLA Ops:
  0.6 55.1 %gather.1 = (f32[512,1024]{1,0:T(8,128)}, f32[512,16,128]{2,1,0:T(8,128)}, f32[512,1024]{1,0:T(8,128)}, f32[512,512]{1,0:T(8,128)}) custom-call(f32[512,16,128]{2,1,0:T(8,128)} %bitcast.6, f32[512,1024]{1,0:T(8,128)} %bitcast.8), custom_call_target="tpu_custom_call" | custom-call | tf_op jit(solution)/shard_map/gather/pallas_call | solution.py:487
  55.8 13.3 %update.1 = (f32[8192,128]{1,0:T(8,128)}, f32[512,1024]{1,0:T(8,128)}) custom-call(f32[512,1024]{1,0:T(8,128)} %get-tuple-element.8.t_hbm, f32[8192,128]{1,0:T(8,128)} %bitcast.10, f32[512,1024]{1,0:T(8,128)} %get-tuple-element.10.r_hbm, f32[512,512]{1,0:T(8,128)} %get-tuple-element.11.a_hbm, f32[8192,128]{1,0:T(8,128)} %bitcast.7, f32[512,1024]{1,0:T(8,128)} %bitcast.9), custom_call_target="tpu_custom_call" | custom-call | tf_op jit(solution)/shard_map/update/pallas_call | solution.py:622

commit v6 on v5

--- a/solution.py
+++ b/solution.py
@@ -119,15 +119,15 @@
             for t in range(4):
                 target = at(STEPS[t][0] + 4, STEPS[t][1] + 4, 1, z)
 
-                @pl.when(n < 16)
-                def _():
-                    block = pl.ds(128 * t + 8 * n, 8)
-                    remote(x_hbm.at[block], f_out.at[block], root_send.at[t], tree_recv.at[t, n], target).start()
-
-                @pl.when(n >= 16)
-                def _():
-                    block = pl.ds(pl.multiple_of(128 * t + 16 * (n - 16), 16), 16)
-                    remote(y_hbm.at[block], y_out.at[block], root_send.at[t + 4], tree_recv.at[t, n], target).start()
+                @pl.when(n < 4)
+                def _():
+                    block = pl.ds(128 * t + 32 * n, 32)
+                    remote(x_hbm.at[block], f_out.at[block], root_send.at[t], tree_recv.at[t, 4 * n], target).start()
+
+                @pl.when(n >= 4)
+                def _():
+                    block = pl.ds(pl.multiple_of(128 * t + 64 * (n - 4), 64), 64)
+                    remote(y_hbm.at[block], y_out.at[block], root_send.at[t + 4], tree_recv.at[t, 4 * n], target).start()
 
             return carry
 
@@ -182,13 +182,17 @@
             @pl.when(k == 0)
             def _():
                 give_tile()
-                feed(0, 13)
+                feed(0, 2)
 
             @pl.when(k == 1)
             def _():
-                feed(13, CHUNKS)
+                feed(2, 4)
 
             @pl.when(k == 2)
+            def _():
+                feed(4, 6)
+
+            @pl.when(k == 3)
             def _():
                 hand_over()
 
@@ -233,7 +237,7 @@
 
         @pl.when(s == 0)
         def _():
-            feed(0, CHUNKS)
+            feed(0, 6)
             hand_over()
 
     quarter = jnp.where(x == 1, 0, jnp.where(y == 1, 1, jnp.where(x == 3, 2, 3)))
@@ -418,7 +422,20 @@
             return at(x + STEPS[d][0] + 4, y + STEPS[d][1] + 4, 1, z)
 
         def flow(kind, t, n, copy):
-            copy(t, n, tree_send.at[kind, 0], tree_recv.at[t, n + 16 * kind], mate).wait_recv()
+            early = starts[t] == HOP
+
+            @pl.when(jnp.logical_not(early))
+            def _():
+                copy(t, n, tree_send.at[kind, 0], tree_recv.at[t, n + 16 * kind], mate).wait_recv()
+
+            @pl.when(jnp.logical_and(early, n % 4 == 0))
+            def _():
+                if kind == 0:
+                    group = f_out.at[pl.ds(128 * t + 8 * n, 32)]
+                else:
+                    group = y_out.at[pl.ds(pl.multiple_of(128 * t + 16 * n, 16), 64)]
+                remote(group, group, tree_send.at[kind, 0], tree_recv.at[t, n + 16 * kind], mate).wait_recv()
+
             for d in range(4):
 
                 @pl.when(gives[t][d])

time: 70.6 us -> 72.7 us (1.030); the launches traced: 69.3 us -> 72.5 us
  Pallas kernels: 68.5 us -> 71.7 us
    pallas_call x1, Pallas kernels: 55.1 us -> 58.4 us  [gather(): pl.pallas_call(gather_kernel, out_shape=(jax.ShapeDtypeStruct((512, 1024)...]
where the time goes in v6:
time: 72.7 us; the launch traced here: 72.5 us
  Pallas kernels  71.7 us (99%)
  between operations  0.82 us (1%)
    pallas_call x1, Pallas kernels, gather(): pl.pallas_call(gather_kernel, out_shape=(jax.ShapeDtypeStruct((512, 1024)...  58.4 us
    pallas_call x1, Pallas kernels, update(): pl.pallas_call(update_kernel, out_shape=(jax.ShapeDtypeStruct((8192, 128)...  13.3 us

profile of v6, /device:TPU:131, one launch (start us, length us, event | category | flops | bytes accessed | tf_op | source)
XLA Modules:
  0.0 72.5 jit_solution(11299863664101217492)
XLA Ops:
  0.6 58.4 %gather.1 = (f32[512,1024]{1,0:T(8,128)}, f32[512,16,128]{2,1,0:T(8,128)}, f32[512,1024]{1,0:T(8,128)}, f32[512,512]{1,0:T(8,128)}) custom-call(f32[512,16,128]{2,1,0:T(8,128)} %bitcast.6, f32[512,1024]{1,0:T(8,128)} %bitcast.8), custom_call_target="tpu_custom_call" | custom-call | tf_op jit(solution)/shard_map/gather/pallas_call | solution.py:504
  59.1 13.3 %update.1 = (f32[8192,128]{1,0:T(8,128)}, f32[512,1024]{1,0:T(8,128)}) custom-call(f32[512,1024]{1,0:T(8,128)} %get-tuple-element.8.t_hbm, f32[8192,128]{1,0:T(8,128)} %bitcast.10, f32[512,1024]{1,0:T(8,128)} %get-tuple-element.10.r_hbm, f32[512,512]{1,0:T(8,128)} %get-tuple-element.11.a_hbm, f32[8192,128]{1,0:T(8,128)} %bitcast.7, f32[512,1024]{1,0:T(8,128)} %bitcast.9), custom_call_target="tpu_custom_call" | custom-call | tf_op jit(solution)/shard_map/update/pallas_call | solution.py:639
